TPU v7x, 256 devices: a whole 4x4x8 slice. The times are simulated.
256 devices in a mesh: blk: 32 (over y_hi, z, core), tm: 8 (over y_lo, x).
Axes of the slice: x: 4, y: 4 (y_hi: 2, y_lo: 2; y = y_hi * 2 + y_lo), z: 8, core: 2. Of those that a mesh axis runs over, the one named last changes fastest.
Arguments:
- waveforms: bfloat16 [480, 131072], P(None, ('blk', 'tm')), may hold values from -60 to 60
- templates: bfloat16 [32, 480, 256], P('blk'), may hold values from -6 to 6
- station_mask: int32 [32, 160], P('blk'), may hold values 0 or 1
- channel_order: int32 [480], replicated, may hold values from 0 to 479, each once
Outputs:
- detection: float32 [32, 131072], P(None, ('blk', 'tm'))
Inputs may be any that keep to these rules, and one draw needn't show every extreme that they name: `channel_order`: each of 0 to 479 appears once.
All inputs are finite; a program needn't handle non-finite values. No bound on the sum of `station_mask` on one device may be relied on, other than what follows from the above.
Results may differ from a plain program's by a relative error of at most 0.0003.
Values may be sent and summed in bfloat16 or wider, within the bound.
A program may use at most 64 MiB of HBM per device.

v0:
```python
import jax
import jax.numpy as jnp
from jax import lax
from jax.sharding import PartitionSpec as P

EPSILON = 1e-05


def shifted(block, axis, distance):
    devices = range(lax.axis_size(axis))
    route = [(i - distance, i) for i in devices if i - distance in devices]
    return lax.ppermute(block, axis, route)


def shifted_2(block, axis, distance):
    devices = range(lax.axis_size(axis))
    route = [((i - distance) % len(devices), i) for i in devices]
    return lax.ppermute(block, axis, route)


def window_sums(squares, window_len):
    running = squares
    window = 1
    while window < window_len:
        columns = running.shape[1]
        running = running[:, : columns - window] + running[:, window:]
        window = window * 2
    return running


def correlate(masked_row, extended, slab_len, window_len):
    products = lax.dot_general(
        masked_row, extended, (((0,), (0,)), ((), ())), preferred_element_type=jnp.float32
    )
    columns = extended.shape[1]
    flattened = jnp.concatenate([products.reshape(-1), jnp.zeros((window_len,), jnp.float32)])
    skewed = flattened.reshape(window_len, columns + 1)[:, :slab_len]
    return jnp.sum(skewed, axis=0)


def prepare(tpl_rows, flag_rows, onehot, window_len):
    channel_mask = jnp.dot(flag_rows.astype(jnp.float32), onehot, precision=lax.Precision.HIGHEST)
    masked = tpl_rows * channel_mask.astype(jnp.bfloat16)[:, :, None]
    tpl_norm = jnp.sqrt(jnp.sum(masked.astype(jnp.float32) ** 2, axis=(1, 2)) + EPSILON)
    live = jnp.sum(channel_mask, axis=1)
    row_scale = jnp.sqrt(window_len * live) / tpl_norm
    return (channel_mask, masked, row_scale)


def on_device(waveforms, templates, station_mask, channel_order):
    window_len = templates.shape[2]
    slab_len = waveforms.shape[1]
    group_rows = templates.shape[0]
    station_count = station_mask.shape[1]
    groups_count = lax.axis_size("blk")
    my_group = lax.axis_index("blk")
    total_rows = group_rows * groups_count
    next_edge = shifted(waveforms[:, : window_len - 1], ("blk", "tm"), -1)
    extended = jnp.concatenate([waveforms, next_edge], axis=1)
    energy = window_sums(extended.astype(jnp.float32) ** 2, window_len)
    station_of = channel_order // 3
    onehot = (jnp.arange(station_count, dtype=jnp.int32)[:, None] == station_of[None, :]).astype(
        jnp.float32
    )
    station_flags = station_mask.astype(jnp.bfloat16)

    def process(carried, tpl_rows, flag_rows, first_row):
        detect_rows, channel_rows = carried
        row_count = tpl_rows.shape[0]
        channel_mask, masked, row_scale = prepare(tpl_rows, flag_rows, onehot, window_len)
        first_row = jnp.asarray(first_row, jnp.int32)

        def one_row(row_index, detect_now):
            masked_row = lax.dynamic_index_in_dim(masked, row_index, 0, keepdims=False)
            corr_row = correlate(masked_row, extended, slab_len, window_len)
            scale_now = lax.dynamic_index_in_dim(row_scale, row_index, 0, keepdims=False)
            target = first_row + row_index
            return lax.dynamic_update_slice(
                detect_now, (corr_row * scale_now)[None, :], (target, jnp.int32(0))
            )

        detect_rows = lax.fori_loop(0, row_count, one_row, detect_rows)
        channel_rows = lax.dynamic_update_slice(
            channel_rows, channel_mask, (first_row, jnp.int32(0))
        )
        return (detect_rows, channel_rows)

    start_state = (
        jnp.zeros((total_rows, slab_len), jnp.float32),
        jnp.zeros((total_rows, extended.shape[0]), jnp.float32),
    )
    carried = process(start_state, templates, station_flags, my_group * group_rows)

    def advance(step_index, loop_state):
        carried_now, tpl_now, flag_now = loop_state
        tpl_now, flag_now = shifted_2((tpl_now, flag_now), "blk", 1)
        owner_group = (my_group - step_index) % groups_count
        carried_now = process(carried_now, tpl_now, flag_now, owner_group * group_rows)
        return (carried_now, tpl_now, flag_now)

    carried = lax.fori_loop(1, groups_count, advance, (carried, templates, station_flags))[0]
    detect_rows, channel_rows = carried
    window_energy = jnp.dot(channel_rows, energy, precision=lax.Precision.HIGHEST)
    return detect_rows / jnp.sqrt(window_energy + EPSILON)


def solution(mesh):
    placed = (P(None, ("blk", "tm")), P("blk", None, None), P("blk", None), P())
    return jax.shard_map(
        on_device, mesh=mesh, in_specs=placed, out_specs=P(None, ("blk", "tm")), check_vma=False
    )
```

profile of v0, /device:TPU:16, one launch (start us, length us, event | category | flops | bytes accessed | tf_op | source)
XLA Modules:
  0.0 459.2 jit_solution(5792771937609500470)
XLA Ops:
  0.0 1.0 copy.26
  1.0 1.0 slice.66
  2.0 9.3 %collective-permute-start.2 = (bf16[480,255]{1,0:T(8,128)(2,1)S(1)}, bf16[480,255]{1,0:T(8,128)(2,1)S(1)}, u32[]{:S(2)}, u32[]{:S(2)}) collective-permute-start(bf16[480,255]{1,0:T(8,128)(2,1)S(1)} %slice.66), channel_id=1, source_target_pairs={{1,0},{2,1},{3,2},{4,3},{5,4},{6,5},{7,6},{8,7},{9,8},{10,9},{11,1... | collective-permute-start | bytes 734408 | tf_op jit(solution)/shard_map/ppermute | solution.py:12
  12.6 0.8 fusion.12
  14.9 0.9 multiply_reduce_fusion.1
  17.3 1.5 reshape.113
  18.8 1.2 concatenate.14
  20.0 1.0 reshape.114
  21.0 1.1 slice_reduce_fusion.1
  24.9 1.4 slice_add_fusion.6
  26.4 430.0 %while.36 = (s32[]{:T(128)}, f32[32,512]{1,0:T(8,128)S(1)}, f32[32,480]{1,0:T(8,128)S(1)}, bf16[1,480,256]{2,1,0:T(8,128)(2,1)S(1)}, bf16[1,160]{1,0:T(2,128)(2,...) while((s32[]{:T(128)}, f32[32,512]{1,0:T(8,128)S(1)}, ...), condition=%wide.region_7.8_spmd.clone, body=%wide.region_3.7_spmd.clone.sunk | while | flops 190319552 | bytes 8754952 | solution.py:101
  26.6 9.2 %collective-permute-done.1 = bf16[1,160]{1,0:T(2,128)(2,1)S(1)} collective-permute-done((bf16[1,160]{1,0:T(2,128)(2,1)S(1)}, bf16[1,160]{1,0:T(2,128)(2,1)S(1)}, u32[]{:S(2)}, u32[]{:S(2)}) %collective-permute-start.1) | collective-permute-done | bytes 352 | tf_op jit(solution)/shard_map/while/body/eval_jaxpr/ppermute | solution.py:18
  37.3 0.8 multiply_reduce_fusion.3
  40.5 9.2 %collective-permute-done.1 = bf16[1,160]{1,0:T(2,128)(2,1)S(1)} collective-permute-done((bf16[1,160]{1,0:T(2,128)(2,1)S(1)}, bf16[1,160]{1,0:T(2,128)(2,1)S(1)}, u32[]{:S(2)}, u32[]{:S(2)}) %collective-permute-start.1) | collective-permute-done | bytes 352 | tf_op jit(solution)/shard_map/while/body/eval_jaxpr/ppermute | solution.py:18
  51.2 0.8 multiply_reduce_fusion.3
  54.3 9.2 %collective-permute-done.1 = bf16[1,160]{1,0:T(2,128)(2,1)S(1)} collective-permute-done((bf16[1,160]{1,0:T(2,128)(2,1)S(1)}, bf16[1,160]{1,0:T(2,128)(2,1)S(1)}, u32[]{:S(2)}, u32[]{:S(2)}) %collective-permute-start.1) | collective-permute-done | bytes 352 | tf_op jit(solution)/shard_map/while/body/eval_jaxpr/ppermute | solution.py:18
  65.0 0.8 multiply_reduce_fusion.3
  68.2 9.2 %collective-permute-done.1 = bf16[1,160]{1,0:T(2,128)(2,1)S(1)} collective-permute-done((bf16[1,160]{1,0:T(2,128)(2,1)S(1)}, bf16[1,160]{1,0:T(2,128)(2,1)S(1)}, u32[]{:S(2)}, u32[]{:S(2)}) %collective-permute-start.1) | collective-permute-done | bytes 352 | tf_op jit(solution)/shard_map/while/body/eval_jaxpr/ppermute | solution.py:18
  78.9 0.8 multiply_reduce_fusion.3
  82.1 9.2 %collective-permute-done.1 = bf16[1,160]{1,0:T(2,128)(2,1)S(1)} collective-permute-done((bf16[1,160]{1,0:T(2,128)(2,1)S(1)}, bf16[1,160]{1,0:T(2,128)(2,1)S(1)}, u32[]{:S(2)}, u32[]{:S(2)}) %collective-permute-start.1) | collective-permute-done | bytes 352 | tf_op jit(solution)/shard_map/while/body/eval_jaxpr/ppermute | solution.py:18
  95.9 9.2 %collective-permute-done.1 = bf16[1,160]{1,0:T(2,128)(2,1)S(1)} collective-permute-done((bf16[1,160]{1,0:T(2,128)(2,1)S(1)}, bf16[1,160]{1,0:T(2,128)(2,1)S(1)}, u32[]{:S(2)}, u32[]{:S(2)}) %collective-permute-start.1) | collective-permute-done | bytes 352 | tf_op jit(solution)/shard_map/while/body/eval_jaxpr/ppermute | solution.py:18
  109.8 9.2 %collective-permute-done.1 = bf16[1,160]{1,0:T(2,128)(2,1)S(1)} collective-permute-done((bf16[1,160]{1,0:T(2,128)(2,1)S(1)}, bf16[1,160]{1,0:T(2,128)(2,1)S(1)}, u32[]{:S(2)}, u32[]{:S(2)}) %collective-permute-start.1) | collective-permute-done | bytes 352 | tf_op jit(solution)/shard_map/while/body/eval_jaxpr/ppermute | solution.py:18
  123.7 9.2 %collective-permute-done.1 = bf16[1,160]{1,0:T(2,128)(2,1)S(1)} collective-permute-done((bf16[1,160]{1,0:T(2,128)(2,1)S(1)}, bf16[1,160]{1,0:T(2,128)(2,1)S(1)}, u32[]{:S(2)}, u32[]{:S(2)}) %collective-permute-start.1) | collective-permute-done | bytes 352 | tf_op jit(solution)/shard_map/while/body/eval_jaxpr/ppermute | solution.py:18
  137.5 9.2 %collective-permute-done.1 = bf16[1,160]{1,0:T(2,128)(2,1)S(1)} collective-permute-done((bf16[1,160]{1,0:T(2,128)(2,1)S(1)}, bf16[1,160]{1,0:T(2,128)(2,1)S(1)}, u32[]{:S(2)}, u32[]{:S(2)}) %collective-permute-start.1) | collective-permute-done | bytes 352 | tf_op jit(solution)/shard_map/while/body/eval_jaxpr/ppermute | solution.py:18
  151.4 9.2 %collective-permute-done.1 = bf16[1,160]{1,0:T(2,128)(2,1)S(1)} collective-permute-done((bf16[1,160]{1,0:T(2,128)(2,1)S(1)}, bf16[1,160]{1,0:T(2,128)(2,1)S(1)}, u32[]{:S(2)}, u32[]{:S(2)}) %collective-permute-start.1) | collective-permute-done | bytes 352 | tf_op jit(solution)/shard_map/while/body/eval_jaxpr/ppermute | solution.py:18
  165.3 9.2 %collective-permute-done.1 = bf16[1,160]{1,0:T(2,128)(2,1)S(1)} collective-permute-done((bf16[1,160]{1,0:T(2,128)(2,1)S(1)}, bf16[1,160]{1,0:T(2,128)(2,1)S(1)}, u32[]{:S(2)}, u32[]{:S(2)}) %collective-permute-start.1) | collective-permute-done | bytes 352 | tf_op jit(solution)/shard_map/while/body/eval_jaxpr/ppermute | solution.py:18
  179.1 9.2 %collective-permute-done.1 = bf16[1,160]{1,0:T(2,128)(2,1)S(1)} collective-permute-done((bf16[1,160]{1,0:T(2,128)(2,1)S(1)}, bf16[1,160]{1,0:T(2,128)(2,1)S(1)}, u32[]{:S(2)}, u32[]{:S(2)}) %collective-permute-start.1) | collective-permute-done | bytes 352 | tf_op jit(solution)/shard_map/while/body/eval_jaxpr/ppermute | solution.py:18
  193.0 9.2 %collective-permute-done.1 = bf16[1,160]{1,0:T(2,128)(2,1)S(1)} collective-permute-done((bf16[1,160]{1,0:T(2,128)(2,1)S(1)}, bf16[1,160]{1,0:T(2,128)(2,1)S(1)}, u32[]{:S(2)}, u32[]{:S(2)}) %collective-permute-start.1) | collective-permute-done | bytes 352 | tf_op jit(solution)/shard_map/while/body/eval_jaxpr/ppermute | solution.py:18
  206.9 9.2 %collective-permute-done.1 = bf16[1,160]{1,0:T(2,128)(2,1)S(1)} collective-permute-done((bf16[1,160]{1,0:T(2,128)(2,1)S(1)}, bf16[1,160]{1,0:T(2,128)(2,1)S(1)}, u32[]{:S(2)}, u32[]{:S(2)}) %collective-permute-start.1) | collective-permute-done | bytes 352 | tf_op jit(solution)/shard_map/while/body/eval_jaxpr/ppermute | solution.py:18
  220.8 9.2 %collective-permute-done.1 = bf16[1,160]{1,0:T(2,128)(2,1)S(1)} collective-permute-done((bf16[1,160]{1,0:T(2,128)(2,1)S(1)}, bf16[1,160]{1,0:T(2,128)(2,1)S(1)}, u32[]{:S(2)}, u32[]{:S(2)}) %collective-permute-start.1) | collective-permute-done | bytes 352 | tf_op jit(solution)/shard_map/while/body/eval_jaxpr/ppermute | solution.py:18
  234.6 9.2 %collective-permute-done.1 = bf16[1,160]{1,0:T(2,128)(2,1)S(1)} collective-permute-done((bf16[1,160]{1,0:T(2,128)(2,1)S(1)}, bf16[1,160]{1,0:T(2,128)(2,1)S(1)}, u32[]{:S(2)}, u32[]{:S(2)}) %collective-permute-start.1) | collective-permute-done | bytes 352 | tf_op jit(solution)/shard_map/while/body/eval_jaxpr/ppermute | solution.py:18
  248.5 9.2 %collective-permute-done.1 = bf16[1,160]{1,0:T(2,128)(2,1)S(1)} collective-permute-done((bf16[1,160]{1,0:T(2,128)(2,1)S(1)}, bf16[1,160]{1,0:T(2,128)(2,1)S(1)}, u32[]{:S(2)}, u32[]{:S(2)}) %collective-permute-start.1) | collective-permute-done | bytes 352 | tf_op jit(solution)/shard_map/while/body/eval_jaxpr/ppermute | solution.py:18
  262.4 9.2 %collective-permute-done.1 = bf16[1,160]{1,0:T(2,128)(2,1)S(1)} collective-permute-done((bf16[1,160]{1,0:T(2,128)(2,1)S(1)}, bf16[1,160]{1,0:T(2,128)(2,1)S(1)}, u32[]{:S(2)}, u32[]{:S(2)}) %collective-permute-start.1) | collective-permute-done | bytes 352 | tf_op jit(solution)/shard_map/while/body/eval_jaxpr/ppermute | solution.py:18
  276.2 9.2 %collective-permute-done.1 = bf16[1,160]{1,0:T(2,128)(2,1)S(1)} collective-permute-done((bf16[1,160]{1,0:T(2,128)(2,1)S(1)}, bf16[1,160]{1,0:T(2,128)(2,1)S(1)}, u32[]{:S(2)}, u32[]{:S(2)}) %collective-permute-start.1) | collective-permute-done | bytes 352 | tf_op jit(solution)/shard_map/while/body/eval_jaxpr/ppermute | solution.py:18
  290.1 9.2 %collective-permute-done.1 = bf16[1,160]{1,0:T(2,128)(2,1)S(1)} collective-permute-done((bf16[1,160]{1,0:T(2,128)(2,1)S(1)}, bf16[1,160]{1,0:T(2,128)(2,1)S(1)}, u32[]{:S(2)}, u32[]{:S(2)}) %collective-permute-start.1) | collective-permute-done | bytes 352 | tf_op jit(solution)/shard_map/while/body/eval_jaxpr/ppermute | solution.py:18
  304.0 9.2 %collective-permute-done.1 = bf16[1,160]{1,0:T(2,128)(2,1)S(1)} collective-permute-done((bf16[1,160]{1,0:T(2,128)(2,1)S(1)}, bf16[1,160]{1,0:T(2,128)(2,1)S(1)}, u32[]{:S(2)}, u32[]{:S(2)}) %collective-permute-start.1) | collective-permute-done | bytes 352 | tf_op jit(solution)/shard_map/while/body/eval_jaxpr/ppermute | solution.py:18
  314.7 0.8 multiply_reduce_fusion.3
  317.8 9.2 %collective-permute-done.1 = bf16[1,160]{1,0:T(2,128)(2,1)S(1)} collective-permute-done((bf16[1,160]{1,0:T(2,128)(2,1)S(1)}, bf16[1,160]{1,0:T(2,128)(2,1)S(1)}, u32[]{:S(2)}, u32[]{:S(2)}) %collective-permute-start.1) | collective-permute-done | bytes 352 | tf_op jit(solution)/shard_map/while/body/eval_jaxpr/ppermute | solution.py:18
  331.7 9.2 %collective-permute-done.1 = bf16[1,160]{1,0:T(2,128)(2,1)S(1)} collective-permute-done((bf16[1,160]{1,0:T(2,128)(2,1)S(1)}, bf16[1,160]{1,0:T(2,128)(2,1)S(1)}, u32[]{:S(2)}, u32[]{:S(2)}) %collective-permute-start.1) | collective-permute-done | bytes 352 | tf_op jit(solution)/shard_map/while/body/eval_jaxpr/ppermute | solution.py:18
  345.6 9.2 %collective-permute-done.1 = bf16[1,160]{1,0:T(2,128)(2,1)S(1)} collective-permute-done((bf16[1,160]{1,0:T(2,128)(2,1)S(1)}, bf16[1,160]{1,0:T(2,128)(2,1)S(1)}, u32[]{:S(2)}, u32[]{:S(2)}) %collective-permute-start.1) | collective-permute-done | bytes 352 | tf_op jit(solution)/shard_map/while/body/eval_jaxpr/ppermute | solution.py:18
  359.5 9.2 %collective-permute-done.1 = bf16[1,160]{1,0:T(2,128)(2,1)S(1)} collective-permute-done((bf16[1,160]{1,0:T(2,128)(2,1)S(1)}, bf16[1,160]{1,0:T(2,128)(2,1)S(1)}, u32[]{:S(2)}, u32[]{:S(2)}) %collective-permute-start.1) | collective-permute-done | bytes 352 | tf_op jit(solution)/shard_map/while/body/eval_jaxpr/ppermute | solution.py:18
  373.3 9.2 %collective-permute-done.1 = bf16[1,160]{1,0:T(2,128)(2,1)S(1)} collective-permute-done((bf16[1,160]{1,0:T(2,128)(2,1)S(1)}, bf16[1,160]{1,0:T(2,128)(2,1)S(1)}, u32[]{:S(2)}, u32[]{:S(2)}) %collective-permute-start.1) | collective-permute-done | bytes 352 | tf_op jit(solution)/shard_map/while/body/eval_jaxpr/ppermute | solution.py:18
  387.2 9.2 %collective-permute-done.1 = bf16[1,160]{1,0:T(2,128)(2,1)S(1)} collective-permute-done((bf16[1,160]{1,0:T(2,128)(2,1)S(1)}, bf16[1,160]{1,0:T(2,128)(2,1)S(1)}, u32[]{:S(2)}, u32[]{:S(2)}) %collective-permute-start.1) | collective-permute-done | bytes 352 | tf_op jit(solution)/shard_map/while/body/eval_jaxpr/ppermute | solution.py:18
  401.1 9.2 %collective-permute-done.1 = bf16[1,160]{1,0:T(2,128)(2,1)S(1)} collective-permute-done((bf16[1,160]{1,0:T(2,128)(2,1)S(1)}, bf16[1,160]{1,0:T(2,128)(2,1)S(1)}, u32[]{:S(2)}, u32[]{:S(2)}) %collective-permute-start.1) | collective-permute-done | bytes 352 | tf_op jit(solution)/shard_map/while/body/eval_jaxpr/ppermute | solution.py:18
  414.9 9.2 %collective-permute-done.1 = bf16[1,160]{1,0:T(2,128)(2,1)S(1)} collective-permute-done((bf16[1,160]{1,0:T(2,128)(2,1)S(1)}, bf16[1,160]{1,0:T(2,128)(2,1)S(1)}, u32[]{:S(2)}, u32[]{:S(2)}) %collective-permute-start.1) | collective-permute-done | bytes 352 | tf_op jit(solution)/shard_map/while/body/eval_jaxpr/ppermute | solution.py:18
  428.8 9.2 %collective-permute-done.1 = bf16[1,160]{1,0:T(2,128)(2,1)S(1)} collective-permute-done((bf16[1,160]{1,0:T(2,128)(2,1)S(1)}, bf16[1,160]{1,0:T(2,128)(2,1)S(1)}, u32[]{:S(2)}, u32[]{:S(2)}) %collective-permute-start.1) | collective-permute-done | bytes 352 | tf_op jit(solution)/shard_map/while/body/eval_jaxpr/ppermute | solution.py:18
  442.7 9.2 %collective-permute-done.1 = bf16[1,160]{1,0:T(2,128)(2,1)S(1)} collective-permute-done((bf16[1,160]{1,0:T(2,128)(2,1)S(1)}, bf16[1,160]{1,0:T(2,128)(2,1)S(1)}, u32[]{:S(2)}, u32[]{:S(2)}) %collective-permute-start.1) | collective-permute-done | bytes 352 | tf_op jit(solution)/shard_map/while/body/eval_jaxpr/ppermute | solution.py:18
  456.3 2.2 fusion.10
  (545 shorter events, 106.4 us)
Async XLA Ops:
  2.0 14.7 %collective-permute-start.2 = (bf16[480,255]{1,0:T(8,128)(2,1)S(1)}, bf16[480,255]{1,0:T(8,128)(2,1)S(1)}, u32[]{:S(2)}, u32[]{:S(2)}) collective-permute-start(bf16[480,255]{1,0:T(8,128)(2,1)S(1)} %slice.66), channel_id=1, source_target_pairs={{1,0},{2,1},{3,2},{4,3},{5,4},{6,5},{7,6},{8,7},{9,8},{10,9},{11,1... | collective-permute-start | bytes 734408 | tf_op jit(solution)/shard_map/ppermute | solution.py:12
  26.4 10.9 %collective-permute-start = (bf16[1,480,256]{2,1,0:T(8,128)(2,1)S(1)}, bf16[1,480,256]{2,1,0:T(8,128)(2,1)S(1)}, u32[]{:S(2)}, u32[]{:S(2)}) collective-permute-start(bf16[1,480,256]{2,1,0:T(8,128)(2,1)S(1)} %get-tuple-element.365), channel_id=1, source_target_pairs={{248,0},{0,8},{8,16},{16,24},{24,32},{32,40},{40,48},{48,56},{56,6... | collective-permute-start | bytes 737288 | tf_op jit(solution)/shard_map/while/body/eval_jaxpr/ppermute | solution.py:18
  26.5 9.3 %collective-permute-start.1 = (bf16[1,160]{1,0:T(2,128)(2,1)S(1)}, bf16[1,160]{1,0:T(2,128)(2,1)S(1)}, u32[]{:S(2)}, u32[]{:S(2)}) collective-permute-start(bf16[1,160]{1,0:T(2,128)(2,1)S(1)} %get-tuple-element.366), channel_id=1, source_target_pairs={{248,0},{0,8},{8,16},{16,24},{24,32},{32,40},{40,48},{48,56},{56,6... | collective-permute-start | bytes 968 | tf_op jit(solution)/shard_map/while/body/eval_jaxpr/ppermute | solution.py:18
  40.2 10.9 %collective-permute-start = (bf16[1,480,256]{2,1,0:T(8,128)(2,1)S(1)}, bf16[1,480,256]{2,1,0:T(8,128)(2,1)S(1)}, u32[]{:S(2)}, u32[]{:S(2)}) collective-permute-start(bf16[1,480,256]{2,1,0:T(8,128)(2,1)S(1)} %get-tuple-element.365), channel_id=1, source_target_pairs={{248,0},{0,8},{8,16},{16,24},{24,32},{32,40},{40,48},{48,56},{56,6... | collective-permute-start | bytes 737288 | tf_op jit(solution)/shard_map/while/body/eval_jaxpr/ppermute | solution.py:18
  40.3 9.3 %collective-permute-start.1 = (bf16[1,160]{1,0:T(2,128)(2,1)S(1)}, bf16[1,160]{1,0:T(2,128)(2,1)S(1)}, u32[]{:S(2)}, u32[]{:S(2)}) collective-permute-start(bf16[1,160]{1,0:T(2,128)(2,1)S(1)} %get-tuple-element.366), channel_id=1, source_target_pairs={{248,0},{0,8},{8,16},{16,24},{24,32},{32,40},{40,48},{48,56},{56,6... | collective-permute-start | bytes 968 | tf_op jit(solution)/shard_map/while/body/eval_jaxpr/ppermute | solution.py:18
  54.1 10.9 %collective-permute-start = (bf16[1,480,256]{2,1,0:T(8,128)(2,1)S(1)}, bf16[1,480,256]{2,1,0:T(8,128)(2,1)S(1)}, u32[]{:S(2)}, u32[]{:S(2)}) collective-permute-start(bf16[1,480,256]{2,1,0:T(8,128)(2,1)S(1)} %get-tuple-element.365), channel_id=1, source_target_pairs={{248,0},{0,8},{8,16},{16,24},{24,32},{32,40},{40,48},{48,56},{56,6... | collective-permute-start | bytes 737288 | tf_op jit(solution)/shard_map/while/body/eval_jaxpr/ppermute | solution.py:18
  54.2 9.3 %collective-permute-start.1 = (bf16[1,160]{1,0:T(2,128)(2,1)S(1)}, bf16[1,160]{1,0:T(2,128)(2,1)S(1)}, u32[]{:S(2)}, u32[]{:S(2)}) collective-permute-start(bf16[1,160]{1,0:T(2,128)(2,1)S(1)} %get-tuple-element.366), channel_id=1, source_target_pairs={{248,0},{0,8},{8,16},{16,24},{24,32},{32,40},{40,48},{48,56},{56,6... | collective-permute-start | bytes 968 | tf_op jit(solution)/shard_map/while/body/eval_jaxpr/ppermute | solution.py:18
  68.0 10.9 %collective-permute-start = (bf16[1,480,256]{2,1,0:T(8,128)(2,1)S(1)}, bf16[1,480,256]{2,1,0:T(8,128)(2,1)S(1)}, u32[]{:S(2)}, u32[]{:S(2)}) collective-permute-start(bf16[1,480,256]{2,1,0:T(8,128)(2,1)S(1)} %get-tuple-element.365), channel_id=1, source_target_pairs={{248,0},{0,8},{8,16},{16,24},{24,32},{32,40},{40,48},{48,56},{56,6... | collective-permute-start | bytes 737288 | tf_op jit(solution)/shard_map/while/body/eval_jaxpr/ppermute | solution.py:18
  68.1 9.3 %collective-permute-start.1 = (bf16[1,160]{1,0:T(2,128)(2,1)S(1)}, bf16[1,160]{1,0:T(2,128)(2,1)S(1)}, u32[]{:S(2)}, u32[]{:S(2)}) collective-permute-start(bf16[1,160]{1,0:T(2,128)(2,1)S(1)} %get-tuple-element.366), channel_id=1, source_target_pairs={{248,0},{0,8},{8,16},{16,24},{24,32},{32,40},{40,48},{48,56},{56,6... | collective-permute-start | bytes 968 | tf_op jit(solution)/shard_map/while/body/eval_jaxpr/ppermute | solution.py:18
  81.9 10.9 %collective-permute-start = (bf16[1,480,256]{2,1,0:T(8,128)(2,1)S(1)}, bf16[1,480,256]{2,1,0:T(8,128)(2,1)S(1)}, u32[]{:S(2)}, u32[]{:S(2)}) collective-permute-start(bf16[1,480,256]{2,1,0:T(8,128)(2,1)S(1)} %get-tuple-element.365), channel_id=1, source_target_pairs={{248,0},{0,8},{8,16},{16,24},{24,32},{32,40},{40,48},{48,56},{56,6... | collective-permute-start | bytes 737288 | tf_op jit(solution)/shard_map/while/body/eval_jaxpr/ppermute | solution.py:18
  81.9 9.3 %collective-permute-start.1 = (bf16[1,160]{1,0:T(2,128)(2,1)S(1)}, bf16[1,160]{1,0:T(2,128)(2,1)S(1)}, u32[]{:S(2)}, u32[]{:S(2)}) collective-permute-start(bf16[1,160]{1,0:T(2,128)(2,1)S(1)} %get-tuple-element.366), channel_id=1, source_target_pairs={{248,0},{0,8},{8,16},{16,24},{24,32},{32,40},{40,48},{48,56},{56,6... | collective-permute-start | bytes 968 | tf_op jit(solution)/shard_map/while/body/eval_jaxpr/ppermute | solution.py:18
  95.7 10.9 %collective-permute-start = (bf16[1,480,256]{2,1,0:T(8,128)(2,1)S(1)}, bf16[1,480,256]{2,1,0:T(8,128)(2,1)S(1)}, u32[]{:S(2)}, u32[]{:S(2)}) collective-permute-start(bf16[1,480,256]{2,1,0:T(8,128)(2,1)S(1)} %get-tuple-element.365), channel_id=1, source_target_pairs={{248,0},{0,8},{8,16},{16,24},{24,32},{32,40},{40,48},{48,56},{56,6... | collective-permute-start | bytes 737288 | tf_op jit(solution)/shard_map/while/body/eval_jaxpr/ppermute | solution.py:18
  95.8 9.3 %collective-permute-start.1 = (bf16[1,160]{1,0:T(2,128)(2,1)S(1)}, bf16[1,160]{1,0:T(2,128)(2,1)S(1)}, u32[]{:S(2)}, u32[]{:S(2)}) collective-permute-start(bf16[1,160]{1,0:T(2,128)(2,1)S(1)} %get-tuple-element.366), channel_id=1, source_target_pairs={{248,0},{0,8},{8,16},{16,24},{24,32},{32,40},{40,48},{48,56},{56,6... | collective-permute-start | bytes 968 | tf_op jit(solution)/shard_map/while/body/eval_jaxpr/ppermute | solution.py:18
  109.6 10.9 %collective-permute-start = (bf16[1,480,256]{2,1,0:T(8,128)(2,1)S(1)}, bf16[1,480,256]{2,1,0:T(8,128)(2,1)S(1)}, u32[]{:S(2)}, u32[]{:S(2)}) collective-permute-start(bf16[1,480,256]{2,1,0:T(8,128)(2,1)S(1)} %get-tuple-element.365), channel_id=1, source_target_pairs={{248,0},{0,8},{8,16},{16,24},{24,32},{32,40},{40,48},{48,56},{56,6... | collective-permute-start | bytes 737288 | tf_op jit(solution)/shard_map/while/body/eval_jaxpr/ppermute | solution.py:18
  109.7 9.3 %collective-permute-start.1 = (bf16[1,160]{1,0:T(2,128)(2,1)S(1)}, bf16[1,160]{1,0:T(2,128)(2,1)S(1)}, u32[]{:S(2)}, u32[]{:S(2)}) collective-permute-start(bf16[1,160]{1,0:T(2,128)(2,1)S(1)} %get-tuple-element.366), channel_id=1, source_target_pairs={{248,0},{0,8},{8,16},{16,24},{24,32},{32,40},{40,48},{48,56},{56,6... | collective-permute-start | bytes 968 | tf_op jit(solution)/shard_map/while/body/eval_jaxpr/ppermute | solution.py:18
  123.5 10.9 %collective-permute-start = (bf16[1,480,256]{2,1,0:T(8,128)(2,1)S(1)}, bf16[1,480,256]{2,1,0:T(8,128)(2,1)S(1)}, u32[]{:S(2)}, u32[]{:S(2)}) collective-permute-start(bf16[1,480,256]{2,1,0:T(8,128)(2,1)S(1)} %get-tuple-element.365), channel_id=1, source_target_pairs={{248,0},{0,8},{8,16},{16,24},{24,32},{32,40},{40,48},{48,56},{56,6... | collective-permute-start | bytes 737288 | tf_op jit(solution)/shard_map/while/body/eval_jaxpr/ppermute | solution.py:18
  123.6 9.3 %collective-permute-start.1 = (bf16[1,160]{1,0:T(2,128)(2,1)S(1)}, bf16[1,160]{1,0:T(2,128)(2,1)S(1)}, u32[]{:S(2)}, u32[]{:S(2)}) collective-permute-start(bf16[1,160]{1,0:T(2,128)(2,1)S(1)} %get-tuple-element.366), channel_id=1, source_target_pairs={{248,0},{0,8},{8,16},{16,24},{24,32},{32,40},{40,48},{48,56},{56,6... | collective-permute-start | bytes 968 | tf_op jit(solution)/shard_map/while/body/eval_jaxpr/ppermute | solution.py:18
  137.3 10.9 %collective-permute-start = (bf16[1,480,256]{2,1,0:T(8,128)(2,1)S(1)}, bf16[1,480,256]{2,1,0:T(8,128)(2,1)S(1)}, u32[]{:S(2)}, u32[]{:S(2)}) collective-permute-start(bf16[1,480,256]{2,1,0:T(8,128)(2,1)S(1)} %get-tuple-element.365), channel_id=1, source_target_pairs={{248,0},{0,8},{8,16},{16,24},{24,32},{32,40},{40,48},{48,56},{56,6... | collective-permute-start | bytes 737288 | tf_op jit(solution)/shard_map/while/body/eval_jaxpr/ppermute | solution.py:18
  137.4 9.3 %collective-permute-start.1 = (bf16[1,160]{1,0:T(2,128)(2,1)S(1)}, bf16[1,160]{1,0:T(2,128)(2,1)S(1)}, u32[]{:S(2)}, u32[]{:S(2)}) collective-permute-start(bf16[1,160]{1,0:T(2,128)(2,1)S(1)} %get-tuple-element.366), channel_id=1, source_target_pairs={{248,0},{0,8},{8,16},{16,24},{24,32},{32,40},{40,48},{48,56},{56,6... | collective-permute-start | bytes 968 | tf_op jit(solution)/shard_map/while/body/eval_jaxpr/ppermute | solution.py:18
  151.2 10.9 %collective-permute-start = (bf16[1,480,256]{2,1,0:T(8,128)(2,1)S(1)}, bf16[1,480,256]{2,1,0:T(8,128)(2,1)S(1)}, u32[]{:S(2)}, u32[]{:S(2)}) collective-permute-start(bf16[1,480,256]{2,1,0:T(8,128)(2,1)S(1)} %get-tuple-element.365), channel_id=1, source_target_pairs={{248,0},{0,8},{8,16},{16,24},{24,32},{32,40},{40,48},{48,56},{56,6... | collective-permute-start | bytes 737288 | tf_op jit(solution)/shard_map/while/body/eval_jaxpr/ppermute | solution.py:18
  151.3 9.3 %collective-permute-start.1 = (bf16[1,160]{1,0:T(2,128)(2,1)S(1)}, bf16[1,160]{1,0:T(2,128)(2,1)S(1)}, u32[]{:S(2)}, u32[]{:S(2)}) collective-permute-start(bf16[1,160]{1,0:T(2,128)(2,1)S(1)} %get-tuple-element.366), channel_id=1, source_target_pairs={{248,0},{0,8},{8,16},{16,24},{24,32},{32,40},{40,48},{48,56},{56,6... | collective-permute-start | bytes 968 | tf_op jit(solution)/shard_map/while/body/eval_jaxpr/ppermute | solution.py:18
  165.1 10.9 %collective-permute-start = (bf16[1,480,256]{2,1,0:T(8,128)(2,1)S(1)}, bf16[1,480,256]{2,1,0:T(8,128)(2,1)S(1)}, u32[]{:S(2)}, u32[]{:S(2)}) collective-permute-start(bf16[1,480,256]{2,1,0:T(8,128)(2,1)S(1)} %get-tuple-element.365), channel_id=1, source_target_pairs={{248,0},{0,8},{8,16},{16,24},{24,32},{32,40},{40,48},{48,56},{56,6... | collective-permute-start | bytes 737288 | tf_op jit(solution)/shard_map/while/body/eval_jaxpr/ppermute | solution.py:18
  165.2 9.3 %collective-permute-start.1 = (bf16[1,160]{1,0:T(2,128)(2,1)S(1)}, bf16[1,160]{1,0:T(2,128)(2,1)S(1)}, u32[]{:S(2)}, u32[]{:S(2)}) collective-permute-start(bf16[1,160]{1,0:T(2,128)(2,1)S(1)} %get-tuple-element.366), channel_id=1, source_target_pairs={{248,0},{0,8},{8,16},{16,24},{24,32},{32,40},{40,48},{48,56},{56,6... | collective-permute-start | bytes 968 | tf_op jit(solution)/shard_map/while/body/eval_jaxpr/ppermute | solution.py:18
  178.9 10.9 %collective-permute-start = (bf16[1,480,256]{2,1,0:T(8,128)(2,1)S(1)}, bf16[1,480,256]{2,1,0:T(8,128)(2,1)S(1)}, u32[]{:S(2)}, u32[]{:S(2)}) collective-permute-start(bf16[1,480,256]{2,1,0:T(8,128)(2,1)S(1)} %get-tuple-element.365), channel_id=1, source_target_pairs={{248,0},{0,8},{8,16},{16,24},{24,32},{32,40},{40,48},{48,56},{56,6... | collective-permute-start | bytes 737288 | tf_op jit(solution)/shard_map/while/body/eval_jaxpr/ppermute | solution.py:18
  179.0 9.3 %collective-permute-start.1 = (bf16[1,160]{1,0:T(2,128)(2,1)S(1)}, bf16[1,160]{1,0:T(2,128)(2,1)S(1)}, u32[]{:S(2)}, u32[]{:S(2)}) collective-permute-start(bf16[1,160]{1,0:T(2,128)(2,1)S(1)} %get-tuple-element.366), channel_id=1, source_target_pairs={{248,0},{0,8},{8,16},{16,24},{24,32},{32,40},{40,48},{48,56},{56,6... | collective-permute-start | bytes 968 | tf_op jit(solution)/shard_map/while/body/eval_jaxpr/ppermute | solution.py:18
  192.8 10.9 %collective-permute-start = (bf16[1,480,256]{2,1,0:T(8,128)(2,1)S(1)}, bf16[1,480,256]{2,1,0:T(8,128)(2,1)S(1)}, u32[]{:S(2)}, u32[]{:S(2)}) collective-permute-start(bf16[1,480,256]{2,1,0:T(8,128)(2,1)S(1)} %get-tuple-element.365), channel_id=1, source_target_pairs={{248,0},{0,8},{8,16},{16,24},{24,32},{32,40},{40,48},{48,56},{56,6... | collective-permute-start | bytes 737288 | tf_op jit(solution)/shard_map/while/body/eval_jaxpr/ppermute | solution.py:18
  192.9 9.3 %collective-permute-start.1 = (bf16[1,160]{1,0:T(2,128)(2,1)S(1)}, bf16[1,160]{1,0:T(2,128)(2,1)S(1)}, u32[]{:S(2)}, u32[]{:S(2)}) collective-permute-start(bf16[1,160]{1,0:T(2,128)(2,1)S(1)} %get-tuple-element.366), channel_id=1, source_target_pairs={{248,0},{0,8},{8,16},{16,24},{24,32},{32,40},{40,48},{48,56},{56,6... | collective-permute-start | bytes 968 | tf_op jit(solution)/shard_map/while/body/eval_jaxpr/ppermute | solution.py:18
  206.7 10.9 %collective-permute-start = (bf16[1,480,256]{2,1,0:T(8,128)(2,1)S(1)}, bf16[1,480,256]{2,1,0:T(8,128)(2,1)S(1)}, u32[]{:S(2)}, u32[]{:S(2)}) collective-permute-start(bf16[1,480,256]{2,1,0:T(8,128)(2,1)S(1)} %get-tuple-element.365), channel_id=1, source_target_pairs={{248,0},{0,8},{8,16},{16,24},{24,32},{32,40},{40,48},{48,56},{56,6... | collective-permute-start | bytes 737288 | tf_op jit(solution)/shard_map/while/body/eval_jaxpr/ppermute | solution.py:18
  206.8 9.3 %collective-permute-start.1 = (bf16[1,160]{1,0:T(2,128)(2,1)S(1)}, bf16[1,160]{1,0:T(2,128)(2,1)S(1)}, u32[]{:S(2)}, u32[]{:S(2)}) collective-permute-start(bf16[1,160]{1,0:T(2,128)(2,1)S(1)} %get-tuple-element.366), channel_id=1, source_target_pairs={{248,0},{0,8},{8,16},{16,24},{24,32},{32,40},{40,48},{48,56},{56,6... | collective-permute-start | bytes 968 | tf_op jit(solution)/shard_map/while/body/eval_jaxpr/ppermute | solution.py:18
  220.5 10.9 %collective-permute-start = (bf16[1,480,256]{2,1,0:T(8,128)(2,1)S(1)}, bf16[1,480,256]{2,1,0:T(8,128)(2,1)S(1)}, u32[]{:S(2)}, u32[]{:S(2)}) collective-permute-start(bf16[1,480,256]{2,1,0:T(8,128)(2,1)S(1)} %get-tuple-element.365), channel_id=1, source_target_pairs={{248,0},{0,8},{8,16},{16,24},{24,32},{32,40},{40,48},{48,56},{56,6... | collective-permute-start | bytes 737288 | tf_op jit(solution)/shard_map/while/body/eval_jaxpr/ppermute | solution.py:18
  220.6 9.3 %collective-permute-start.1 = (bf16[1,160]{1,0:T(2,128)(2,1)S(1)}, bf16[1,160]{1,0:T(2,128)(2,1)S(1)}, u32[]{:S(2)}, u32[]{:S(2)}) collective-permute-start(bf16[1,160]{1,0:T(2,128)(2,1)S(1)} %get-tuple-element.366), channel_id=1, source_target_pairs={{248,0},{0,8},{8,16},{16,24},{24,32},{32,40},{40,48},{48,56},{56,6... | collective-permute-start | bytes 968 | tf_op jit(solution)/shard_map/while/body/eval_jaxpr/ppermute | solution.py:18
  234.4 10.9 %collective-permute-start = (bf16[1,480,256]{2,1,0:T(8,128)(2,1)S(1)}, bf16[1,480,256]{2,1,0:T(8,128)(2,1)S(1)}, u32[]{:S(2)}, u32[]{:S(2)}) collective-permute-start(bf16[1,480,256]{2,1,0:T(8,128)(2,1)S(1)} %get-tuple-element.365), channel_id=1, source_target_pairs={{248,0},{0,8},{8,16},{16,24},{24,32},{32,40},{40,48},{48,56},{56,6... | collective-permute-start | bytes 737288 | tf_op jit(solution)/shard_map/while/body/eval_jaxpr/ppermute | solution.py:18
  234.5 9.3 %collective-permute-start.1 = (bf16[1,160]{1,0:T(2,128)(2,1)S(1)}, bf16[1,160]{1,0:T(2,128)(2,1)S(1)}, u32[]{:S(2)}, u32[]{:S(2)}) collective-permute-start(bf16[1,160]{1,0:T(2,128)(2,1)S(1)} %get-tuple-element.366), channel_id=1, source_target_pairs={{248,0},{0,8},{8,16},{16,24},{24,32},{32,40},{40,48},{48,56},{56,6... | collective-permute-start | bytes 968 | tf_op jit(solution)/shard_map/while/body/eval_jaxpr/ppermute | solution.py:18
  248.3 10.9 %collective-permute-start = (bf16[1,480,256]{2,1,0:T(8,128)(2,1)S(1)}, bf16[1,480,256]{2,1,0:T(8,128)(2,1)S(1)}, u32[]{:S(2)}, u32[]{:S(2)}) collective-permute-start(bf16[1,480,256]{2,1,0:T(8,128)(2,1)S(1)} %get-tuple-element.365), channel_id=1, source_target_pairs={{248,0},{0,8},{8,16},{16,24},{24,32},{32,40},{40,48},{48,56},{56,6... | collective-permute-start | bytes 737288 | tf_op jit(solution)/shard_map/while/body/eval_jaxpr/ppermute | solution.py:18
  262.2 10.9 %collective-permute-start = (bf16[1,480,256]{2,1,0:T(8,128)(2,1)S(1)}, bf16[1,480,256]{2,1,0:T(8,128)(2,1)S(1)}, u32[]{:S(2)}, u32[]{:S(2)}) collective-permute-start(bf16[1,480,256]{2,1,0:T(8,128)(2,1)S(1)} %get-tuple-element.365), channel_id=1, source_target_pairs={{248,0},{0,8},{8,16},{16,24},{24,32},{32,40},{40,48},{48,56},{56,6... | collective-permute-start | bytes 737288 | tf_op jit(solution)/shard_map/while/body/eval_jaxpr/ppermute | solution.py:18
  276.0 10.9 %collective-permute-start = (bf16[1,480,256]{2,1,0:T(8,128)(2,1)S(1)}, bf16[1,480,256]{2,1,0:T(8,128)(2,1)S(1)}, u32[]{:S(2)}, u32[]{:S(2)}) collective-permute-start(bf16[1,480,256]{2,1,0:T(8,128)(2,1)S(1)} %get-tuple-element.365), channel_id=1, source_target_pairs={{248,0},{0,8},{8,16},{16,24},{24,32},{32,40},{40,48},{48,56},{56,6... | collective-permute-start | bytes 737288 | tf_op jit(solution)/shard_map/while/body/eval_jaxpr/ppermute | solution.py:18
  289.9 10.9 %collective-permute-start = (bf16[1,480,256]{2,1,0:T(8,128)(2,1)S(1)}, bf16[1,480,256]{2,1,0:T(8,128)(2,1)S(1)}, u32[]{:S(2)}, u32[]{:S(2)}) collective-permute-start(bf16[1,480,256]{2,1,0:T(8,128)(2,1)S(1)} %get-tuple-element.365), channel_id=1, source_target_pairs={{248,0},{0,8},{8,16},{16,24},{24,32},{32,40},{40,48},{48,56},{56,6... | collective-permute-start | bytes 737288 | tf_op jit(solution)/shard_map/while/body/eval_jaxpr/ppermute | solution.py:18
  303.8 10.9 %collective-permute-start = (bf16[1,480,256]{2,1,0:T(8,128)(2,1)S(1)}, bf16[1,480,256]{2,1,0:T(8,128)(2,1)S(1)}, u32[]{:S(2)}, u32[]{:S(2)}) collective-permute-start(bf16[1,480,256]{2,1,0:T(8,128)(2,1)S(1)} %get-tuple-element.365), channel_id=1, source_target_pairs={{248,0},{0,8},{8,16},{16,24},{24,32},{32,40},{40,48},{48,56},{56,6... | collective-permute-start | bytes 737288 | tf_op jit(solution)/shard_map/while/body/eval_jaxpr/ppermute | solution.py:18
  317.6 10.9 %collective-permute-start = (bf16[1,480,256]{2,1,0:T(8,128)(2,1)S(1)}, bf16[1,480,256]{2,1,0:T(8,128)(2,1)S(1)}, u32[]{:S(2)}, u32[]{:S(2)}) collective-permute-start(bf16[1,480,256]{2,1,0:T(8,128)(2,1)S(1)} %get-tuple-element.365), channel_id=1, source_target_pairs={{248,0},{0,8},{8,16},{16,24},{24,32},{32,40},{40,48},{48,56},{56,6... | collective-permute-start | bytes 737288 | tf_op jit(solution)/shard_map/while/body/eval_jaxpr/ppermute | solution.py:18
  331.5 10.9 %collective-permute-start = (bf16[1,480,256]{2,1,0:T(8,128)(2,1)S(1)}, bf16[1,480,256]{2,1,0:T(8,128)(2,1)S(1)}, u32[]{:S(2)}, u32[]{:S(2)}) collective-permute-start(bf16[1,480,256]{2,1,0:T(8,128)(2,1)S(1)} %get-tuple-element.365), channel_id=1, source_target_pairs={{248,0},{0,8},{8,16},{16,24},{24,32},{32,40},{40,48},{48,56},{56,6... | collective-permute-start | bytes 737288 | tf_op jit(solution)/shard_map/while/body/eval_jaxpr/ppermute | solution.py:18
  345.4 10.9 %collective-permute-start = (bf16[1,480,256]{2,1,0:T(8,128)(2,1)S(1)}, bf16[1,480,256]{2,1,0:T(8,128)(2,1)S(1)}, u32[]{:S(2)}, u32[]{:S(2)}) collective-permute-start(bf16[1,480,256]{2,1,0:T(8,128)(2,1)S(1)} %get-tuple-element.365), channel_id=1, source_target_pairs={{248,0},{0,8},{8,16},{16,24},{24,32},{32,40},{40,48},{48,56},{56,6... | collective-permute-start | bytes 737288 | tf_op jit(solution)/shard_map/while/body/eval_jaxpr/ppermute | solution.py:18
  359.2 10.9 %collective-permute-start = (bf16[1,480,256]{2,1,0:T(8,128)(2,1)S(1)}, bf16[1,480,256]{2,1,0:T(8,128)(2,1)S(1)}, u32[]{:S(2)}, u32[]{:S(2)}) collective-permute-start(bf16[1,480,256]{2,1,0:T(8,128)(2,1)S(1)} %get-tuple-element.365), channel_id=1, source_target_pairs={{248,0},{0,8},{8,16},{16,24},{24,32},{32,40},{40,48},{48,56},{56,6... | collective-permute-start | bytes 737288 | tf_op jit(solution)/shard_map/while/body/eval_jaxpr/ppermute | solution.py:18
  373.1 10.9 %collective-permute-start = (bf16[1,480,256]{2,1,0:T(8,128)(2,1)S(1)}, bf16[1,480,256]{2,1,0:T(8,128)(2,1)S(1)}, u32[]{:S(2)}, u32[]{:S(2)}) collective-permute-start(bf16[1,480,256]{2,1,0:T(8,128)(2,1)S(1)} %get-tuple-element.365), channel_id=1, source_target_pairs={{248,0},{0,8},{8,16},{16,24},{24,32},{32,40},{40,48},{48,56},{56,6... | collective-permute-start | bytes 737288 | tf_op jit(solution)/shard_map/while/body/eval_jaxpr/ppermute | solution.py:18
  387.0 10.9 %collective-permute-start = (bf16[1,480,256]{2,1,0:T(8,128)(2,1)S(1)}, bf16[1,480,256]{2,1,0:T(8,128)(2,1)S(1)}, u32[]{:S(2)}, u32[]{:S(2)}) collective-permute-start(bf16[1,480,256]{2,1,0:T(8,128)(2,1)S(1)} %get-tuple-element.365), channel_id=1, source_target_pairs={{248,0},{0,8},{8,16},{16,24},{24,32},{32,40},{40,48},{48,56},{56,6... | collective-permute-start | bytes 737288 | tf_op jit(solution)/shard_map/while/body/eval_jaxpr/ppermute | solution.py:18
  400.9 10.9 %collective-permute-start = (bf16[1,480,256]{2,1,0:T(8,128)(2,1)S(1)}, bf16[1,480,256]{2,1,0:T(8,128)(2,1)S(1)}, u32[]{:S(2)}, u32[]{:S(2)}) collective-permute-start(bf16[1,480,256]{2,1,0:T(8,128)(2,1)S(1)} %get-tuple-element.365), channel_id=1, source_target_pairs={{248,0},{0,8},{8,16},{16,24},{24,32},{32,40},{40,48},{48,56},{56,6... | collective-permute-start | bytes 737288 | tf_op jit(solution)/shard_map/while/body/eval_jaxpr/ppermute | solution.py:18
  414.7 10.9 %collective-permute-start = (bf16[1,480,256]{2,1,0:T(8,128)(2,1)S(1)}, bf16[1,480,256]{2,1,0:T(8,128)(2,1)S(1)}, u32[]{:S(2)}, u32[]{:S(2)}) collective-permute-start(bf16[1,480,256]{2,1,0:T(8,128)(2,1)S(1)} %get-tuple-element.365), channel_id=1, source_target_pairs={{248,0},{0,8},{8,16},{16,24},{24,32},{32,40},{40,48},{48,56},{56,6... | collective-permute-start | bytes 737288 | tf_op jit(solution)/shard_map/while/body/eval_jaxpr/ppermute | solution.py:18
  428.6 10.9 %collective-permute-start = (bf16[1,480,256]{2,1,0:T(8,128)(2,1)S(1)}, bf16[1,480,256]{2,1,0:T(8,128)(2,1)S(1)}, u32[]{:S(2)}, u32[]{:S(2)}) collective-permute-start(bf16[1,480,256]{2,1,0:T(8,128)(2,1)S(1)} %get-tuple-element.365), channel_id=1, source_target_pairs={{248,0},{0,8},{8,16},{16,24},{24,32},{32,40},{40,48},{48,56},{56,6... | collective-permute-start | bytes 737288 | tf_op jit(solution)/shard_map/while/body/eval_jaxpr/ppermute | solution.py:18
  442.5 10.9 %collective-permute-start = (bf16[1,480,256]{2,1,0:T(8,128)(2,1)S(1)}, bf16[1,480,256]{2,1,0:T(8,128)(2,1)S(1)}, u32[]{:S(2)}, u32[]{:S(2)}) collective-permute-start(bf16[1,480,256]{2,1,0:T(8,128)(2,1)S(1)} %get-tuple-element.365), channel_id=1, source_target_pairs={{248,0},{0,8},{8,16},{16,24},{24,32},{32,40},{40,48},{48,56},{56,6... | collective-permute-start | bytes 737288 | tf_op jit(solution)/shard_map/while/body/eval_jaxpr/ppermute | solution.py:18
  (16 other events, 155.7 us)
where the time goes:
time: 462 us; the launch traced here: 459 us
  waiting for transfers between devices  284 us (61%)
  other arithmetic  53.9 us (12%)
  loops' own time  42 us (9%)
  local copies, waits for them, and re-layouts  36.5 us (8%)
  matrix products  26.9 us (6%)
  starting transfers between devices  14.4 us (3%)
    ppermute x62, waiting for transfers between devices, shifted_2(): return lax.ppermute(block, axis, route)  284 us
    another operation x1, loops' own time, on_device(): lax.fori_loop(1, groups_count, advance, (carried, templates, station_flags))  42 us
    reduce_sum x32, other arithmetic, prepare(): jnp.sum(masked.astype(jnp.float32) ** 2, axis=(1, 2)) + EPSILON  25.3 us
    reshape x32, local copies, waits for them, and re-layouts, correlate(): products.reshape(-1)  21.1 us
    reduce_sum x32, other arithmetic, prepare(): live = jnp.sum(channel_mask, axis=1)  19.1 us
    dot_general x32, matrix products, correlate(): lax.dot_general(masked_row, extended, (((0,), (0,)), ((), ())), preferred...  16 us
    ppermute x1, starting transfers between devices, shifted(): return lax.ppermute(block, axis, route)  9.29 us
  transfers between devices with their start and end apart: 63, of which 31 were waited for; matrix products, arithmetic and copies ran while one was open for 7% of the time, Pallas kernels for 0%

commit v1 on v0

v1 whole, which is shorter than its diff:
```python
import jax
import jax.numpy as jnp
from jax import lax
from jax.experimental import pallas as pl
from jax.experimental.pallas import tpu as pltpu
from jax.sharding import PartitionSpec as P

EPSILON = 1e-05
MESH = pl.DeviceIdType.MESH
F32 = jnp.float32
BF16 = jnp.bfloat16

NX, NY, NZ = 4, 4, 8
CHANNELS, WINDOW, SLAB = 480, 256, 512
LANES = 512
SPAN = SLAB + WINDOW
STEP = 16
ROWS = SLAB + STEP
GROUP = 16
PADDED = 640

REACH = {"C": (4, 3), "A": (3, 4), "B": (4, 3), "I": (3, 4)}
ORDER = (
    ("I", 1), ("C", 1), ("A", 1), ("I", 2), ("C", 2), ("B", 1), ("I", 3), ("C", 3), ("A", 2), ("I", 4), ("C", 4),
    ("A", 3), ("B", 2), ("A", 4), ("B", 3), ("B", 4),
)


def padded_lanes(block):
    return jnp.concatenate([block, jnp.zeros((block.shape[0], LANES - block.shape[1]), block.dtype)], axis=1)


def station_onehot(order):
    first = 3 * lax.broadcasted_iota(jnp.int32, (256, CHANNELS), 0)
    hit = jnp.logical_and(order >= first, order < first + 3)
    return padded_lanes(jnp.where(hit, 1.0, 0.0).astype(F32)).astype(BF16)


def window_energy(mask, block):
    wide = block.astype(F32)
    squares = wide * wide
    high = squares.astype(BF16)
    low = (squares - high.astype(F32)).astype(BF16)
    total = jnp.dot(mask, high, preferred_element_type=F32) + jnp.dot(mask, low, preferred_element_type=F32)
    shift = 1
    while shift < WINDOW:
        total = total + pltpu.roll(total, SPAN - shift, 1)
        shift = shift * 2
    return total[:, :SLAB]


def diagonal_sums(partial):
    turned = partial.T.reshape(GROUP, 2, 8, PADDED)
    low, high = turned[:, 0].reshape(GROUP * 8, PADDED), turned[:, 1].reshape(GROUP * 8, PADDED)
    both = low + pltpu.roll(high, PADDED - 8, 1)
    row = lax.broadcasted_iota(jnp.int32, (GROUP * 8, PADDED), 0)
    for bit in (4, 2, 1):
        both = jnp.where((row & bit) != 0, pltpu.roll(both, PADDED - bit, 1), both)
    return jnp.sum(both.reshape(GROUP, 8, PADDED)[:, :, :SLAB], axis=1)


def kernel(wave_ref, tpl_ref, flag_ref, order_ref, out_ref, g, info, xt, own_halo, sib_wave, sib_halo, part, energy, ready, arrived, ssem, rsem):
    blk, tm = lax.axis_index("blk"), lax.axis_index("tm")
    core, z, h = blk % 2, (blk // 2) % NZ, blk // 16
    x, low_y = tm % NX, tm // NX
    y = 2 * h + low_y
    parity, color = (x + y) % 2, (2 * x + y) % 4

    def device(px, py, pz, pc):
        px, py, pz = (px + NX) % NX, (py + NY) % NY, (pz + NZ) % NZ
        return ((py // 2 * NZ + pz) * 2 + pc, py % 2 * NX + px)

    east, west = device(x + 1, y, z, core), device(x - 1, y, z, core)
    north, south = device(x, y + 1, z, core), device(x, y - 1, z, core)
    up, down = device(x, y, z + 1, core), device(x, y, z - 1, core)
    sibling = device(x, y, z, 1 - core)
    mate = device(x, y + 1 - 2 * low_y, z, core)
    cross = device(x, y + 2 * low_y - 1, z, core)
    place = blk * 8 + tm
    after, before = (place + 1) % 256, (place + 255) % 256
    after, before = (after // 8, after % 8), (before // 8, before % 8)

    barrier = pltpu.get_barrier_semaphore()
    friends = (east, west, north, south, up, down, sibling, after, before)
    for friend in friends:
        pl.semaphore_signal(barrier, inc=1, device_id=friend, device_id_type=MESH)

    slots, sent = {}, []

    def copy(name, source, target, to):
        slot = slots.setdefault(name, len(slots))
        return pltpu.make_async_remote_copy(
            src_ref=source, dst_ref=target, send_sem=ssem.at[slot], recv_sem=rsem.at[slot], device_id=to, device_id_type=MESH
        )

    def send(name, source, to, target=None):
        made = copy(name, source, source if target is None else target, to)
        made.start()
        sent.append(made)

    def receive(name, target):
        copy(name, target, target, sibling).wait_recv()

    order = order_ref[...]
    onehot = station_onehot(order)
    flags = jnp.concatenate([flag_ref[...].astype(F32), jnp.zeros((1, 96), F32)], axis=1)
    mask_row = jnp.dot(jnp.broadcast_to(flags, (16, 256)).astype(BF16), onehot, preferred_element_type=F32)[0:1]
    masked = padded_lanes(tpl_ref[...].T) * mask_row.astype(BF16)
    g[h, z] = masked
    wide = masked.astype(F32)
    norm = jnp.sum(jnp.sum(wide * wide, axis=0, keepdims=True), axis=1, keepdims=True)
    live = jnp.sum(mask_row, axis=1, keepdims=True)
    scale = jnp.sqrt(WINDOW * live) / jnp.sqrt(norm + EPSILON)
    info[h, z] = jnp.concatenate(
        [flags[:, :128], flags[:, 128:], jnp.broadcast_to(scale, (1, 128)), jnp.zeros((5, 128), F32)], axis=0
    )
    pl.semaphore_wait(barrier, len(friends))

    def rows(kind, turn=0, flip=0):
        if kind == "C":
            start = 128 + 32 * ((color + turn) % 4)
        else:
            start = 64 * ((parity + flip) % 2) + (32 if kind == "B" else 0)
        return pl.ds(pl.multiple_of(start, 32), 32)

    def piece(kind, hs, zt, turn=0, flip=0):
        if kind == "I":
            return info.at[hs, zt]
        return g.at[hs, zt, rows(kind, turn, flip), :]

    def own_send(kind, hs, tag):
        send((kind, "+", tag), piece(kind, hs, z), up)
        send((kind, "-", tag), piece(kind, hs, z), down)

    cross_turn = 3 - 2 * low_y
    other = 1 - h
    own_send("I", h, 1)
    own_send("C", h, 1)
    send("cross I", info.at[h, z], cross)
    send("cross C", g.at[h, z, rows("C", cross_turn), :], cross)
    send("wave", wave_ref, sibling, sib_wave)
    send("halo", wave_ref.at[:, pl.ds(0, WINDOW)], before, own_halo)
    half = lambda flip: pl.ds(pl.multiple_of(64 * ((parity + flip) % 2), 64), 64)
    send("cross AB", g.at[h, z, half(1), :], cross)
    own_send("A", h, 1)
    own_send("B", h, 1)
    send("cross BA", g.at[h, z, half(0), :], cross)
    for turn in (1, 2, 3):
        send(("cross C", turn), g.at[h, z, rows("C", cross_turn + turn), :], cross)

    xt[0, 0:SLAB, :] = padded_lanes(wave_ref[...].T)
    receive("wave", sib_wave)
    xt[1, 0:SLAB, :] = padded_lanes(sib_wave[...].T)

    receive("cross I", info.at[other, z])
    own_send("I", other, 0)
    receive("cross C", g.at[other, z, rows("C"), :])
    own_send("C", other, 0)
    receive("cross AB", g.at[other, z, half(0), :])
    own_send("A", other, 0)
    own_send("B", other, 0)

    receive("halo", own_halo)
    send("sib halo", own_halo, sibling, sib_halo)
    edge = jnp.where(place == 255, jnp.zeros((), BF16), own_halo[...])
    xt[0, SLAB:SPAN, :] = padded_lanes(edge.T)

    both = pl.ds(0, 2)
    plane = {"C": [], "A": [], "B": []}

    def push(kind, label, to, zt, turn=0):
        send((kind, label), piece(kind, both, zt), to)

    def zstep(kind, r):
        for sign, name, onward in ((1, "+", up), (-1, "-", down)):
            reach = REACH[kind][0 if sign > 0 else 1]
            if r > reach:
                continue
            zt = (z + 8 - sign * r) % NZ
            if r == 1:
                receive((kind, name, 1), piece(kind, h, zt))
                receive((kind, name, 0), piece(kind, other, zt))
            else:
                receive((kind, name, r), piece(kind, both, zt))
            if r < reach:
                send((kind, name, r + 1), piece(kind, both, zt), onward)
            s = 2 * (r - 1) + (0 if sign > 0 else 1)
            if kind == "I":
                continue
            pushes = {
                "C": [("north", north, 3, 0), ("south", south, 1, 0), ("east" if s % 2 else "west", east if s % 2 else west, 2, 0)],
                "A": [("east", east, 0, 1)],
                "B": [("mate", mate, 0, 1) if s % 2 == 0 else ("west", west, 0, 1)],
            }[kind]
            for side, to, turn, flip in pushes:
                label = (kind, side, name, r)
                send(label, piece(kind, both, zt), to)
                plane[kind].append((label, zt, turn, flip))

    def finish(kind):
        for label, zt, turn, flip in plane[kind]:
            receive(label, piece(kind, both, zt, turn, flip))
        if kind == "C":
            for turn in (1, 2, 3):
                receive(("cross C", turn), g.at[other, z, rows("C", turn), :])
        if kind == "A":
            receive("cross BA", g.at[other, z, half(1), :])

    started = set()

    def multiply(start, slab):
        total = None
        for j in (start // STEP, start // STEP + 1):
            tpl = g[:, :, STEP * j : STEP * (j + 1), :].reshape(GROUP * STEP, LANES)
            term = lax.dot_general(
                xt[slab, STEP * j : STEP * j + ROWS, :], tpl, (((1,), (1,)), ((), ())), preferred_element_type=F32
            )
            total = term if total is None else total + term
        if slab in started:
            part[slab, 0:ROWS, :] += total
        else:
            started.add(slab)
            part[slab, 0:ROWS, :] = total
            part[slab, ROWS:PADDED, :] = jnp.zeros((PADDED - ROWS, GROUP * STEP), F32)

    def energies():
        receive("sib halo", sib_halo)
        sib_place = place + 8 - 16 * core
        sib_edge = jnp.where(sib_place == 255, jnp.zeros((), BF16), sib_halo[...])
        xt[1, SLAB:SPAN, :] = padded_lanes(sib_edge.T)
        gathered = jnp.concatenate(
            [info[:, :, 0, :].reshape(GROUP, 128), info[:, :, 1, :].reshape(GROUP, 128)], axis=1
        ).astype(BF16)
        masks = jnp.dot(gathered, onehot, preferred_element_type=F32).astype(BF16)[:, :CHANNELS]
        gains = info[:, :, 2, :].reshape(GROUP, 128)[:, 0:1]
        for slab, block in ((0, jnp.concatenate([wave_ref[...], edge], axis=1)), (1, jnp.concatenate([sib_wave[...], sib_edge], axis=1))):
            energy[slab] = gains / jnp.sqrt(window_energy(masks, block) + EPSILON)

    work = {
        ("C", 4): ["finish C", "energies"],
        ("A", 3): [(128, 0), (160, 0)],
        ("B", 2): [(192, 0), (224, 0)],
        ("A", 4): [(128, 1), (160, 1)],
        ("B", 3): [(192, 1), (224, 1)],
        ("B", 4): ["finish A", (0, 0), (64, 0), (0, 1), (64, 1), "finish B", (32, 1), (96, 1)],
    }
    for item in ORDER:
        zstep(*item)
        for task in work.get(item, ()):
            if task == "energies":
                energies()
            elif isinstance(task, str):
                finish(task[-1])
            else:
                multiply(*task)

    ready[...] = diagonal_sums(part[1]) * energy[1]
    send("result", ready, sibling, arrived)
    multiply(32, 0)
    multiply(96, 0)
    out_ref[core] = diagonal_sums(part[0]) * energy[0]
    receive("result", arrived)
    out_ref[1 - core] = arrived[...]
    for made in sent:
        made.wait_send()


def on_device(waveforms, templates, station_mask, channel_order):
    vmem = pl.BlockSpec(memory_space=pltpu.VMEM)
    slots = 160
    result = pl.pallas_call(
        kernel,
        out_shape=jax.ShapeDtypeStruct((2, GROUP, SLAB), F32),
        in_specs=[vmem] * 4,
        out_specs=vmem,
        scratch_shapes=[
            pltpu.VMEM((2, NZ, WINDOW, LANES), BF16),
            pltpu.VMEM((2, NZ, 8, 128), F32),
            pltpu.VMEM((2, SPAN, LANES), BF16),
            pltpu.VMEM((CHANNELS, WINDOW), BF16),
            pltpu.VMEM((CHANNELS, SLAB), BF16),
            pltpu.VMEM((CHANNELS, WINDOW), BF16),
            pltpu.VMEM((2, PADDED, GROUP * STEP), F32),
            pltpu.VMEM((2, GROUP, SLAB), F32),
            pltpu.VMEM((GROUP, SLAB), F32),
            pltpu.VMEM((GROUP, SLAB), F32),
            pltpu.SemaphoreType.DMA((slots,)),
            pltpu.SemaphoreType.DMA((slots,)),
        ],
        compiler_params=pltpu.CompilerParams(
            collective_id=0, has_side_effects=True, vmem_limit_bytes=50 * 2**20
        ),
    )(waveforms, templates[0], station_mask, channel_order[None, :])
    return jnp.transpose(result, (1, 0, 2)).reshape(2 * GROUP, SLAB)


def solution(mesh):
    placed = (P(None, ("blk", "tm")), P("blk", None, None), P("blk", None), P())
    return jax.shard_map(
        on_device, mesh=mesh, in_specs=placed, out_specs=P(None, ("blk", "tm")), check_vma=False
    )
```

time: 462 us -> 56.3 us (0.12)
  the two profiles are of different devices: /device:TPU:16 before, /device:TPU:1 now
where the time goes in v1:
time: 56.3 us; the launch traced here: 56.2 us
  Pallas kernels  52.7 us (94%)
  local copies, waits for them, and re-layouts  3.4 us (6%)
    pallas_call x1, Pallas kernels, on_device(): pl.pallas_call(kernel, out_shape=jax.ShapeDtypeStruct((2, GROUP, SLAB), F...  52.7 us
    unnamed x8, local copies, waits for them, and re-layouts  2.67 us

profile of v1, /device:TPU:1, one launch (start us, length us, event | category | flops | bytes accessed | tf_op | source)
XLA Modules:
  0.0 56.2 jit_solution(6937874445470361823)
XLA Ops:
  0.0 0.0 copy-start.2
  0.0 0.0 copy-start.3
  0.0 0.7 %copy-done.2 = s32[480]{0:T(512)S(1)} copy-done((s32[480]{0:T(512)S(1)}, s32[480]{0:T(512)}, u32[]{:S(2)}) %copy-start.2) | copy-done | bytes 1944
  0.7 0.0 copy-done.3
  0.7 0.0 copy-start
  0.7 1.0 %copy-done = bf16[480,512]{1,0:T(8,128)(2,1)S(1)} copy-done((bf16[480,512]{1,0:T(8,128)(2,1)S(1)}, bf16[480,512]{1,0:T(8,128)(2,1)}, u32[]{:S(2)}) %copy-start) | copy-done | bytes 491544
  1.7 0.0 copy-start.1
  1.7 0.9 %copy-done.1 = bf16[1,480,256]{2,1,0:T(8,128)(2,1)S(1)} copy-done((bf16[1,480,256]{2,1,0:T(8,128)(2,1)S(1)}, bf16[1,480,256]{2,1,0:T(8,128)(2,1)}, u32[]{:S(2)}) %copy-start.1) | copy-done | bytes 245784
  2.7 52.7 %shard_map.46 = f32[2,16,512]{2,1,0:T(8,128)S(1)} custom-call(bf16[480,512]{1,0:T(8,128)(2,1)S(1)} %copy-done, bf16[480,256]{1,0:T(8,128)(2,1)S(1)} %bitcast.4, s32[1,160]{1,0:T(1,128)S(1)} %copy-done.3, s32[1,480]{1,0:T(1,128)S(1)} %bitcast.5), custom_call_target="tpu_custom_call" | custom-call | tf_op jit(solution)/shard_map/pallas_call | solution.py:271
  55.4 0.1 copy.5
  55.5 0.7 %reshape.3 = f32[32,512]{1,0:T(8,128)} reshape(f32[16,2,512]{2,1,0:T(2,128)S(1)} %copy.5) | data formatting | bytes 131072 | tf_op jit(solution)/shard_map/reshape | solution.py:294
Async XLA Ops:
  0.0 0.7 %copy-start.2 = (s32[480]{0:T(512)S(1)}, s32[480]{0:T(512)}, u32[]{:S(2)}) copy-start(s32[480]{0:T(512)} %param.7) | copy-start | bytes 5764
  0.0 0.7 %copy-start.3 = (s32[1,160]{1,0:T(1,128)S(1)}, s32[1,160]{1,0:T(1,128)}, u32[]{:S(2)}) copy-start(s32[1,160]{1,0:T(1,128)} %flag_ref.1) | copy-start | bytes 1924
  0.7 1.0 %copy-start = (bf16[480,512]{1,0:T(8,128)(2,1)S(1)}, bf16[480,512]{1,0:T(8,128)(2,1)}, u32[]{:S(2)}) copy-start(bf16[480,512]{1,0:T(8,128)(2,1)} %wave_ref.1) | copy-start | bytes 1474564
  1.7 0.9 %copy-start.1 = (bf16[1,480,256]{2,1,0:T(8,128)(2,1)S(1)}, bf16[1,480,256]{2,1,0:T(8,128)(2,1)}, u32[]{:S(2)}) copy-start(bf16[1,480,256]{2,1,0:T(8,128)(2,1)} %param.5) | copy-start | bytes 737284

commit v2 on v1

v2 whole, which is shorter than its diff:
```python
import jax
import jax.numpy as jnp
from jax import lax
from jax.experimental import pallas as pl
from jax.experimental.pallas import tpu as pltpu
from jax.sharding import PartitionSpec as P

EPSILON = 1e-05
MESH = pl.DeviceIdType.MESH
F32 = jnp.float32
BF16 = jnp.bfloat16

NX, NY, NZ = 4, 4, 8
CHANNELS, WINDOW, SLAB = 480, 256, 512
LANES = 512
SPAN = SLAB + WINDOW
STEP = 16
ROWS = SLAB + STEP
GROUP = 16
PADDED = 640

def padded_lanes(block):
    return jnp.concatenate([block, jnp.zeros((block.shape[0], LANES - block.shape[1]), block.dtype)], axis=1)


def station_onehot(order):
    first = 3 * lax.broadcasted_iota(jnp.int32, (256, CHANNELS), 0)
    hit = jnp.logical_and(order >= first, order < first + 3)
    return padded_lanes(jnp.where(hit, 1.0, 0.0).astype(F32)).astype(BF16)


def window_energy(mask, block):
    wide = block.astype(F32)
    squares = wide * wide
    high = squares.astype(BF16)
    low = (squares - high.astype(F32)).astype(BF16)
    total = jnp.dot(mask, high, preferred_element_type=F32) + jnp.dot(mask, low, preferred_element_type=F32)
    shift = 1
    while shift < WINDOW:
        total = total + pltpu.roll(total, SPAN - shift, 1)
        shift = shift * 2
    return total[:, :SLAB]


def diagonal_sums(partial):
    turned = partial.T.reshape(GROUP, 2, 8, PADDED)
    low, high = turned[:, 0].reshape(GROUP * 8, PADDED), turned[:, 1].reshape(GROUP * 8, PADDED)
    both = low + pltpu.roll(high, PADDED - 8, 1)
    row = lax.broadcasted_iota(jnp.int32, (GROUP * 8, PADDED), 0)
    for bit in (4, 2, 1):
        both = jnp.where((row & bit) != 0, pltpu.roll(both, PADDED - bit, 1), both)
    return jnp.sum(both.reshape(GROUP, 8, PADDED)[:, :, :SLAB], axis=1)


def kernel(
    wave_ref, tpl_ref, flag_ref, order_ref, out_ref,
    g, info, xt, tpl_v, wave_v, halo_v, part, energy, result, arrived, ssem, rsem, lsem, late,
):
    blk, tm = lax.axis_index("blk"), lax.axis_index("tm")
    core, z, h = blk % 2, (blk // 2) % NZ, blk // 16
    x, low_y = tm % NX, tm // NX
    y = 2 * h + low_y
    other = 1 - h
    color = (x + 2 * y) % 4

    def device(px, py, pz, pc):
        px, py, pz = (px + NX) % NX, (py + NY) % NY, (pz + NZ) % NZ
        return ((py // 2 * NZ + pz) * 2 + pc, py % 2 * NX + px)

    cross_y = y + 2 * low_y - 1
    line = {dz: device(x, y, z + dz, core) for dz in (1, -1, 2, -2, 3, -3, 4)}
    cross = {dz: device(x, cross_y, z + dz, core) for dz in (0, 1, -1, 2, -2, 3, -3, 4)}
    east, west = device(x + 1, y, z, core), device(x - 1, y, z, core)
    mate = device(x, y + 1 - 2 * low_y, z, core)
    sibling = device(x, y, z, 1 - core)
    place = blk * 8 + tm
    after, before = (place + 1) % 256, (place + 255) % 256
    after, before = (after // 8, after % 8), (before // 8, before % 8)

    load_tpl = pltpu.make_async_copy(tpl_ref, tpl_v, lsem.at[0])
    load_wave = pltpu.make_async_copy(wave_ref, wave_v.at[core], lsem.at[1])
    load_tpl.start()
    load_wave.start()

    last_in_run = jnp.logical_and(x == NX - 1, low_y == 1)
    first_in_run = jnp.logical_and(x == 0, low_y == 0)
    barrier = pltpu.get_barrier_semaphore()
    friends = list(line.values()) + list(cross.values()) + [east, west, mate]
    for friend in friends:
        pl.semaphore_signal(barrier, inc=1, device_id=friend, device_id_type=MESH)

    @pl.when(core == 0)
    def _():
        pl.semaphore_signal(barrier, inc=1, device_id=sibling, device_id_type=MESH)

    @pl.when(jnp.logical_or(core == 0, jnp.logical_not(last_in_run)))
    def _():
        pl.semaphore_signal(barrier, inc=1, device_id=after, device_id_type=MESH)

    @pl.when(jnp.logical_or(core == 0, jnp.logical_not(first_in_run)))
    def _():
        pl.semaphore_signal(barrier, inc=1, device_id=before, device_id_type=MESH)

    slots, sent = {}, []

    def copy(name, source, target, to):
        slot = slots.setdefault(name, len(slots))
        return pltpu.make_async_remote_copy(
            src_ref=source, dst_ref=target, send_sem=ssem.at[slot], recv_sem=rsem.at[slot], device_id=to, device_id_type=MESH
        )

    def send(name, source, to):
        made = copy(name, source, source, to)
        made.start()
        sent.append(made)

    def receive(name, target):
        copy(name, target, target, sibling).wait_recv()

    order = order_ref[...]
    onehot = station_onehot(order)
    flags = jnp.concatenate([flag_ref[...].astype(F32), jnp.zeros((1, 96), F32)], axis=1)
    mask_row = jnp.dot(jnp.broadcast_to(flags, (16, 256)).astype(BF16), onehot, preferred_element_type=F32)[0:1]
    load_tpl.wait()
    masked = padded_lanes(tpl_v[...].T) * mask_row.astype(BF16)
    g[h, z] = masked
    wide = masked.astype(F32)
    norm = jnp.sum(jnp.sum(wide * wide, axis=0, keepdims=True), axis=1, keepdims=True)
    live = jnp.sum(mask_row, axis=1, keepdims=True)
    scale = jnp.sqrt(WINDOW * live) / jnp.sqrt(norm + EPSILON)
    info[h, z] = jnp.concatenate(
        [flags[:, :128], flags[:, 128:], jnp.broadcast_to(scale, (1, 128)), jnp.zeros((5, 128), F32)], axis=0
    )
    number = lambda yes: jnp.where(yes, 1, 0)
    pl.semaphore_wait(
        barrier,
        len(friends) + core + number(jnp.logical_or(core == 1, jnp.logical_not(last_in_run)))
        + number(jnp.logical_or(core == 1, jnp.logical_not(first_in_run))),
    )

    @pl.when(core == 1)
    def _():
        pl.semaphore_signal(late.at[0], inc=1, device_id=sibling, device_id_type=MESH)

    @pl.when(jnp.logical_and(core == 1, last_in_run))
    def _():
        pl.semaphore_signal(late.at[1], inc=1, device_id=after, device_id_type=MESH)

    def rows(kind, turn):
        return pl.ds(pl.multiple_of(128 * kind + 32 * ((color + turn) % 4), 32), 32)

    def piece(kind, hs, dz, turn=0):
        return g.at[hs, (z - dz + NZ) % NZ, rows(kind, turn), :]

    both = pl.ds(0, 2)
    for kind in (0, 1):
        for dz in (2, -2, 1, -1):
            send((kind, "line", dz), piece(kind, h, 0), line[dz])
            send((kind, "cross", dz), piece(kind, h, 0, 2), cross[dz])
        if kind == 0:
            for dz in line:
                send(("info", "line", dz), info.at[h, z], line[dz])
            for dz in cross:
                send(("info", "cross", dz), info.at[h, z], cross[dz])
    send("cross whole", g.at[h, z], cross[0])

    load_wave.wait()
    wave_copy = copy("wave", wave_v.at[core], wave_v.at[core], sibling)
    halo_copy = copy("halo", wave_v.at[core, :, pl.ds(0, WINDOW)], halo_v.at[core], before)
    edge_copy = copy("edge", wave_v.at[core, :, pl.ds(0, WINDOW)], halo_v.at[1 - core], before)
    crossing = jnp.logical_and(first_in_run, core == 0)

    @pl.when(core == 1)
    def _():
        wave_copy.start()

    @pl.when(jnp.logical_not(first_in_run))
    def _():
        halo_copy.start()

    @pl.when(jnp.logical_and(first_in_run, core == 1))
    def _():
        edge_copy.start()

    plane = {0: [], 1: []}

    def zstep(kind, dz):
        if abs(dz) <= 2:
            receive((kind, "line", dz), piece(kind, h, dz))
            receive((kind, "cross", dz), piece(kind, other, dz))
        else:
            receive((kind, "far", dz), piece(kind, both, dz))
        sign = 1 if dz > 0 else -1
        if abs(dz) == 2:
            send((kind, "far", 3 * sign), piece(kind, both, dz), line[sign])
            if sign == (1 if kind == 0 else -1):
                send((kind, "far", 4), piece(kind, both, dz), line[2 * sign])
        to, label = (mate, "mate") if kind == 0 or dz not in (1, 2, 3) else (cross[0], "cross y")
        for label, to, turn in (("east", east, 3), ("west", west, 1), (label, to, 2)):
            send((kind, label, "plane", dz), piece(kind, both, dz), to)
            plane[kind].append(((kind, label, "plane", dz), dz, turn))

    for step in ((0, 2), (0, -2), (0, 1), (0, -1), (1, 2), (1, -2), (1, 1), (1, -1), (0, 3), (0, -3), (0, 4), (1, 3), (1, -3), (1, 4)):
        zstep(*step)

    @pl.when(core == 0)
    def _():
        pl.semaphore_wait(late.at[0], 1)
        wave_copy.start()

    @pl.when(crossing)
    def _():
        pl.semaphore_wait(late.at[1], 1)
        edge_copy.start()

    @pl.when(jnp.logical_not(last_in_run))
    def _():
        receive("halo", halo_v.at[core])

    @pl.when(last_in_run)
    def _():
        receive("edge", halo_v.at[core])

    send("sib halo", halo_v.at[core], sibling)

    @pl.when(core == 1)
    def _():
        receive("wave", wave_v.at[0])
        receive("sib halo", halo_v.at[0])

    for dz in line:
        receive(("info", "line", dz), info.at[h, (z - dz + NZ) % NZ])
    for dz in cross:
        receive(("info", "cross", dz), info.at[other, (z - dz + NZ) % NZ])
    gathered = jnp.concatenate(
        [info[:, :, 0, :].reshape(GROUP, 128), info[:, :, 1, :].reshape(GROUP, 128)], axis=1
    ).astype(BF16)
    masks = jnp.dot(gathered, onehot, preferred_element_type=F32).astype(BF16)[:, :CHANNELS]
    gains = info[:, :, 2, :].reshape(GROUP, 128)[:, 0:1]

    def prepare(slab):
        wave = wave_v[slab]
        end = place + 8 * (slab - core) == 255
        edge = jnp.where(end, jnp.zeros((), BF16), halo_v[slab])
        xt[slab, 0:SLAB, :] = padded_lanes(wave.T)
        xt[slab, SLAB:SPAN, :] = padded_lanes(edge.T)
        total = window_energy(masks, jnp.concatenate([wave, edge], axis=1))
        energy[slab] = gains / jnp.sqrt(total + EPSILON)

    def multiply(kind, turn, slab, first):
        start = 128 * kind + 32 * ((color + turn) % 4)
        total = None
        for half in (0, STEP):
            at = pl.multiple_of(start + half, STEP)
            tpl = g[:, :, pl.ds(at, STEP), :].reshape(GROUP * STEP, LANES)
            term = lax.dot_general(
                xt[slab, pl.ds(at, ROWS), :], tpl, (((1,), (1,)), ((), ())), preferred_element_type=F32
            )
            total = term if total is None else total + term
        if first:
            part[slab, 0:ROWS, :] = total
            part[slab, ROWS:PADDED, :] = jnp.zeros((PADDED - ROWS, GROUP * STEP), F32)
        else:
            part[slab, 0:ROWS, :] += total

    def finish(kind, turn):
        for name, dz, its in plane[kind]:
            if its == turn:
                receive(name, piece(kind, both, dz, turn))

    prepare(0)
    receive("cross whole", g.at[other, z])
    for kind in (0, 1):
        for turn in (0, 2, 1, 3):
            finish(kind, turn)
            multiply(kind, turn, 0, (kind, turn) == (0, 0))
    result[0] = diagonal_sums(part[0]) * energy[0]
    result_copy = copy("result", result.at[1 - core], arrived, sibling)

    @pl.when(core == 1)
    def _():
        result_copy.start()

    @pl.when(core == 0)
    def _():
        receive("wave", wave_v.at[1])
        receive("sib halo", halo_v.at[1])

    prepare(1)
    for kind in (0, 1):
        for turn in (0, 2, 1, 3):
            multiply(kind, turn, 1, (kind, turn) == (0, 0))
    result[1] = diagonal_sums(part[1]) * energy[1]

    @pl.when(core == 0)
    def _():
        result_copy.start()

    out_ref[core] = result[core]
    receive("result", arrived)
    out_ref[1 - core] = arrived[...]
    for made in sent:
        made.wait_send()
    wave_copy.wait_send()
    result_copy.wait_send()

    @pl.when(jnp.logical_not(first_in_run))
    def _():
        halo_copy.wait_send()

    @pl.when(first_in_run)
    def _():
        edge_copy.wait_send()


def on_device(waveforms, templates, station_mask, channel_order):
    vmem = pl.BlockSpec(memory_space=pltpu.VMEM)
    hbm = pl.BlockSpec(memory_space=pl.ANY)
    slots = 96
    result = pl.pallas_call(
        kernel,
        out_shape=jax.ShapeDtypeStruct((2, GROUP, SLAB), F32),
        in_specs=[hbm, hbm, vmem, vmem],
        out_specs=vmem,
        scratch_shapes=[
            pltpu.VMEM((2, NZ, WINDOW, LANES), BF16),
            pltpu.VMEM((2, NZ, 8, 128), F32),
            pltpu.VMEM((2, SPAN, LANES), BF16),
            pltpu.VMEM((CHANNELS, WINDOW), BF16),
            pltpu.VMEM((2, CHANNELS, SLAB), BF16),
            pltpu.VMEM((2, CHANNELS, WINDOW), BF16),
            pltpu.VMEM((2, PADDED, GROUP * STEP), F32),
            pltpu.VMEM((2, GROUP, SLAB), F32),
            pltpu.VMEM((2, GROUP, SLAB), F32),
            pltpu.VMEM((GROUP, SLAB), F32),
            pltpu.SemaphoreType.DMA((slots,)),
            pltpu.SemaphoreType.DMA((slots,)),
            pltpu.SemaphoreType.DMA((2,)),
            pltpu.SemaphoreType.REGULAR((2,)),
        ],
        compiler_params=pltpu.CompilerParams(
            collective_id=0, has_side_effects=True, vmem_limit_bytes=50 * 2**20
        ),
    )(waveforms, templates[0], station_mask, channel_order[None, :])
    return jnp.transpose(result, (1, 0, 2)).reshape(2 * GROUP, SLAB)


def solution(mesh):
    placed = (P(None, ("blk", "tm")), P("blk", None, None), P("blk", None), P())
    return jax.shard_map(
        on_device, mesh=mesh, in_specs=placed, out_specs=P(None, ("blk", "tm")), check_vma=False
    )
```

time: 56.3 us -> 52.9 us (0.940)
  Pallas kernels: 52.7 us -> 48.9 us
    pallas_call x1, Pallas kernels: 52.7 us -> 48.9 us  [on_device(): pl.pallas_call(kernel, out_shape=jax.ShapeDtypeStruct((2, GROUP, SLAB), F...]
where the time goes in v2:
time: 52.9 us; the launch traced here: 52.3 us
  Pallas kernels  48.9 us (92%)
  local copies, waits for them, and re-layouts  3.4 us (6%)
    pallas_call x1, Pallas kernels, on_device(): pl.pallas_call(kernel, out_shape=jax.ShapeDtypeStruct((2, GROUP, SLAB), F...  48.9 us
    unnamed x8, local copies, waits for them, and re-layouts  2.67 us

profile of v2, /device:TPU:1, one launch (start us, length us, event | category | flops | bytes accessed | tf_op | source)
XLA Modules:
  0.0 52.3 jit_solution(17340413367533955082)
XLA Ops:
  0.0 0.0 copy-start.2
  0.0 0.0 copy-start.3
  0.0 0.7 %copy-done.2 = s32[480]{0:T(512)S(1)} copy-done((s32[480]{0:T(512)S(1)}, s32[480]{0:T(512)}, u32[]{:S(2)}) %copy-start.2) | copy-done | bytes 1944
  0.7 0.0 copy-done.3
  0.7 0.0 copy-start
  0.7 1.0 %copy-done = bf16[480,512]{1,0:T(8,128)(2,1)S(1)} copy-done((bf16[480,512]{1,0:T(8,128)(2,1)S(1)}, bf16[480,512]{1,0:T(8,128)(2,1)}, u32[]{:S(2)}) %copy-start) | copy-done | bytes 491544
  1.7 0.0 copy-start.1
  1.7 0.9 %copy-done.1 = bf16[1,480,256]{2,1,0:T(8,128)(2,1)S(1)} copy-done((bf16[1,480,256]{2,1,0:T(8,128)(2,1)S(1)}, bf16[1,480,256]{2,1,0:T(8,128)(2,1)}, u32[]{:S(2)}) %copy-start.1) | copy-done | bytes 245784
  2.7 48.9 %shard_map.46 = f32[2,16,512]{2,1,0:T(8,128)S(1)} custom-call(bf16[480,512]{1,0:T(8,128)(2,1)S(1)} %copy-done, bf16[480,256]{1,0:T(8,128)(2,1)S(1)} %bitcast.4, s32[1,160]{1,0:T(1,128)S(1)} %copy-done.3, s32[1,480]{1,0:T(1,128)S(1)} %bitcast.5), custom_call_target="tpu_custom_call" | custom-call | tf_op jit(solution)/shard_map/pallas_call | solution.py:320
  51.6 0.1 copy.5
  51.7 0.7 %reshape.3 = f32[32,512]{1,0:T(8,128)} reshape(f32[16,2,512]{2,1,0:T(2,128)S(1)} %copy.5) | data formatting | bytes 131072 | tf_op jit(solution)/shard_map/reshape | solution.py:345
Async XLA Ops:
  0.0 0.7 %copy-start.2 = (s32[480]{0:T(512)S(1)}, s32[480]{0:T(512)}, u32[]{:S(2)}) copy-start(s32[480]{0:T(512)} %param.7) | copy-start | bytes 5764
  0.0 0.7 %copy-start.3 = (s32[1,160]{1,0:T(1,128)S(1)}, s32[1,160]{1,0:T(1,128)}, u32[]{:S(2)}) copy-start(s32[1,160]{1,0:T(1,128)} %flag_ref.1) | copy-start | bytes 1924
  0.7 1.0 %copy-start = (bf16[480,512]{1,0:T(8,128)(2,1)S(1)}, bf16[480,512]{1,0:T(8,128)(2,1)}, u32[]{:S(2)}) copy-start(bf16[480,512]{1,0:T(8,128)(2,1)} %wave_ref.1) | copy-start | bytes 1474564
  1.7 0.9 %copy-start.1 = (bf16[1,480,256]{2,1,0:T(8,128)(2,1)S(1)}, bf16[1,480,256]{2,1,0:T(8,128)(2,1)}, u32[]{:S(2)}) copy-start(bf16[1,480,256]{2,1,0:T(8,128)(2,1)} %param.5) | copy-start | bytes 737284

commit v3 on v2

v3 whole, which is shorter than its diff:
```python
import jax
import jax.numpy as jnp
from jax import lax
from jax.experimental import pallas as pl
from jax.experimental.pallas import tpu as pltpu
from jax.sharding import PartitionSpec as P

EPSILON = 1e-05
MESH = pl.DeviceIdType.MESH
F32 = jnp.float32
BF16 = jnp.bfloat16

NX, NY, NZ = 4, 4, 8
CHANNELS, WINDOW, SLAB = 480, 256, 512
LANES = 512
SPAN = SLAB + WINDOW
STEP = 16
ROWS = SLAB + STEP
GROUP = 16
PADDED = 640

def padded_lanes(block):
    return jnp.concatenate([block, jnp.zeros((block.shape[0], LANES - block.shape[1]), block.dtype)], axis=1)


def station_onehot(order):
    first = 3 * lax.broadcasted_iota(jnp.int32, (256, CHANNELS), 0)
    hit = jnp.logical_and(order >= first, order < first + 3)
    return padded_lanes(jnp.where(hit, 1.0, 0.0).astype(F32)).astype(BF16)


def window_energy(mask, block):
    wide = block.astype(F32)
    squares = wide * wide
    high = squares.astype(BF16)
    low = (squares - high.astype(F32)).astype(BF16)
    total = jnp.dot(mask, high, preferred_element_type=F32) + jnp.dot(mask, low, preferred_element_type=F32)
    shift = 1
    while shift < WINDOW:
        total = total + pltpu.roll(total, SPAN - shift, 1)
        shift = shift * 2
    return total[:, :SLAB]


def diagonal_sums(partial):
    turned = partial.T.reshape(GROUP, 2, 8, PADDED)
    low, high = turned[:, 0].reshape(GROUP * 8, PADDED), turned[:, 1].reshape(GROUP * 8, PADDED)
    both = low + pltpu.roll(high, PADDED - 8, 1)
    row = lax.broadcasted_iota(jnp.int32, (GROUP * 8, PADDED), 0)
    for bit in (4, 2, 1):
        both = jnp.where((row & bit) != 0, pltpu.roll(both, PADDED - bit, 1), both)
    return jnp.sum(both.reshape(GROUP, 8, PADDED)[:, :, :SLAB], axis=1)


def kernel(
    wave_ref, tpl_ref, flag_ref, order_ref, out_ref,
    g, info, xt, order_v, flag_v, tpl_v, wave_v, halo_v, part, energy, result, arrived, ssem, rsem, lsem,
):
    blk, tm = lax.axis_index("blk"), lax.axis_index("tm")
    core, z, h = blk % 2, (blk // 2) % NZ, blk // 16
    x, low_y = tm % NX, tm // NX
    y = 2 * h + low_y
    other = 1 - h
    colors = ((x + 2 * y) % 4, (2 * x + y) % 4)
    cross_turns = (2, 3 - 2 * low_y)

    def device(px, py, pz, pc):
        px, py, pz = (px + NX) % NX, (py + NY) % NY, (pz + NZ) % NZ
        return ((py // 2 * NZ + pz) * 2 + pc, py % 2 * NX + px)

    line = {dz: device(x, y, z + dz, core) for dz in (1, -1, 2, -2)}
    cross = device(x, y + 2 * low_y - 1, z, core)
    east, west = device(x + 1, y, z, core), device(x - 1, y, z, core)
    north, south = device(x, y + 1, z, core), device(x, y - 1, z, core)
    mate = device(x, y + 1 - 2 * low_y, z, core)
    sibling = device(x, y, z, 1 - core)
    place = blk * 8 + tm
    after, before = (place + 1) % 256, (place + 255) % 256
    after, before = (after // 8, after % 8), (before // 8, before % 8)

    load_tpl = pltpu.make_async_copy(tpl_ref, tpl_v, lsem.at[0])
    load_wave = pltpu.make_async_copy(wave_ref, wave_v.at[0], lsem.at[1])
    load_order = pltpu.make_async_copy(order_ref, order_v, lsem.at[2])
    load_flags = pltpu.make_async_copy(flag_ref, flag_v, lsem.at[3])
    load_order.start()
    load_flags.start()
    load_tpl.start()
    load_wave.start()

    barrier = pltpu.get_barrier_semaphore()
    friends = list(line.values()) + [cross, east, west, mate, sibling, after, before]
    for friend in friends:
        pl.semaphore_signal(barrier, inc=1, device_id=friend, device_id_type=MESH)

    slots, sent = {}, []

    def copy(name, source, target, to):
        slot = slots.setdefault(name, len(slots))
        return pltpu.make_async_remote_copy(
            src_ref=source, dst_ref=target, send_sem=ssem.at[slot], recv_sem=rsem.at[slot], device_id=to, device_id_type=MESH
        )

    def send(name, source, to, target=None):
        made = copy(name, source, source if target is None else target, to)
        made.start()
        sent.append(made)

    def receive(name, target):
        copy(name, target, target, sibling).wait_recv()

    load_order.wait()
    load_flags.wait()
    order = order_v[...]
    onehot = station_onehot(order)
    flags = jnp.concatenate([flag_v[...].astype(F32), jnp.zeros((1, 96), F32)], axis=1)
    mask_row = jnp.dot(jnp.broadcast_to(flags, (16, 256)).astype(BF16), onehot, preferred_element_type=F32)[0:1]
    load_tpl.wait()
    masked = padded_lanes(tpl_v[...].T) * mask_row.astype(BF16)
    g[h, z] = masked
    wide = masked.astype(F32)
    norm = jnp.sum(jnp.sum(wide * wide, axis=0, keepdims=True), axis=1, keepdims=True)
    live = jnp.sum(mask_row, axis=1, keepdims=True)
    scale = jnp.sqrt(WINDOW * live) / jnp.sqrt(norm + EPSILON)
    info[h, z] = jnp.concatenate(
        [flags[:, :128], flags[:, 128:], jnp.broadcast_to(scale, (1, 128)), jnp.zeros((5, 128), F32)], axis=0
    )
    load_wave.wait()
    pl.semaphore_wait(barrier, len(friends))

    def rows(kind, turn):
        return pl.ds(pl.multiple_of(128 * kind + 32 * ((colors[kind] + turn) % 4), 32), 32)

    def piece(kind, hs, dz, turn=0):
        return g.at[hs, (z - dz + NZ) % NZ, rows(kind, turn), :]

    both = pl.ds(0, 2)
    send("halo", wave_v.at[0, :, pl.ds(0, WINDOW)], before, halo_v.at[0])
    send("wave", wave_v.at[0], sibling, wave_v.at[1])
    for kind in (0, 1):
        send(("cross", kind, 0), piece(kind, h, 0, cross_turns[kind]), cross)
    send(("cross", "info"), info.at[h, z], cross)

    def to_line(kind, hs, tag):
        for dz in (2, -2, 1, -1):
            if kind == "info":
                send((kind, tag, dz), info.at[hs, z], line[dz])
            else:
                send((kind, tag, dz), piece(kind, hs, 0), line[dz])

    to_line(0, h, "own")
    to_line("info", h, "own")
    to_line(1, h, "own")
    for turn in (1, 2, 3):
        for kind in (0, 1):
            send(("cross", kind, turn), piece(kind, h, 0, cross_turns[kind] + turn), cross)

    plane = {0: [], 1: []}

    def part_of(kind, hs, dz):
        return info.at[hs, (z - dz + NZ) % NZ] if kind == "info" else piece(kind, hs, dz)

    def zstep(kind, dz):
        if abs(dz) <= 2:
            receive((kind, "own", dz), part_of(kind, h, dz))
            receive((kind, "other", dz), part_of(kind, other, dz))
        else:
            receive((kind, "far", dz), part_of(kind, both, dz))
        sign = 1 if dz > 0 else -1
        if abs(dz) == 2:
            send((kind, "far", 3 * sign), part_of(kind, both, dz), line[sign])
            if sign == (1 if kind == 0 else -1):
                send((kind, "far", 4), part_of(kind, both, dz), line[2 * sign])
        if kind == "info":
            return
        if kind == 0:
            pushes = (("east", east, 3), ("west", west, 1), (("cross y", cross, 2) if dz in (2, 1) else ("mate", mate, 2)))
        else:
            third = ("west", west, 2) if dz in (2, -1) else ("east", east, 2)
            pushes = (("north", north, 3), ("south", south, 1), third)
        for label, to, turn in pushes:
            send((kind, label, "plane", dz), piece(kind, both, dz), to)
            plane[kind].append(((kind, label, "plane", dz), dz, turn))

    def multiply(kind, turn, slab, first=False):
        start = 128 * kind + 32 * ((colors[kind] + turn) % 4)
        total = None
        for half in (0, STEP):
            at = pl.multiple_of(start + half, STEP)
            tpl = g[:, :, pl.ds(at, STEP), :].reshape(GROUP * STEP, LANES)
            term = lax.dot_general(
                xt[slab, pl.ds(at, ROWS), :], tpl, (((1,), (1,)), ((), ())), preferred_element_type=F32
            )
            total = term if total is None else total + term
        if first:
            part[slab, 0:ROWS, :] = total
            part[slab, ROWS:PADDED, :] = jnp.zeros((PADDED - ROWS, GROUP * STEP), F32)
        else:
            part[slab, 0:ROWS, :] += total

    def finish(kind, turn):
        for name, dz, its in plane[kind]:
            if its == turn:
                receive(name, piece(kind, both, dz, turn))

    for kind in (0, 1):
        receive(("cross", kind, 0), piece(kind, other, 0))
        to_line(kind, other, "other")
        if kind == 0:
            receive(("cross", "info"), info.at[other, z])
            to_line("info", other, "other")
    xt[0, 0:SLAB, :] = padded_lanes(wave_v[0].T)
    receive("wave", wave_v.at[1])
    xt[1, 0:SLAB, :] = padded_lanes(wave_v[1].T)
    for step in ((0, 2), (0, -2), ("info", 2), ("info", -2), (0, 1), (0, -1), (1, 2), (1, -2), (1, 1), (1, -1), ("info", 1), ("info", -1)):
        zstep(*step)
    receive("halo", halo_v.at[0])
    send("sib halo", halo_v.at[0], sibling, halo_v.at[1])
    edges = [jnp.where(place == 255, jnp.zeros((), BF16), halo_v[0])]
    xt[0, SLAB:SPAN, :] = padded_lanes(edges[0].T)
    for step in ((0, 3), (0, -3), (0, 4)):
        zstep(*step)
    receive("sib halo", halo_v.at[1])
    edges.append(jnp.where(place + 8 - 16 * core == 255, jnp.zeros((), BF16), halo_v[1]))
    xt[1, SLAB:SPAN, :] = padded_lanes(edges[1].T)
    for turn in (1, 2, 3):
        receive(("cross", 0, turn), piece(0, other, 0, turn))
    for slab in (1, 0):
        multiply(0, 0, slab, True)
    for step in ((1, 3), (1, -3), (1, 4), ("info", 3), ("info", -3), ("info", 4)):
        zstep(*step)

    for turn in (1, 2, 3):
        receive(("cross", 1, turn), piece(1, other, 0, turn))
    gathered = jnp.concatenate(
        [info[:, :, 0, :].reshape(GROUP, 128), info[:, :, 1, :].reshape(GROUP, 128)], axis=1
    ).astype(BF16)
    masks = jnp.dot(gathered, onehot, preferred_element_type=F32).astype(BF16)[:, :CHANNELS]
    gains = info[:, :, 2, :].reshape(GROUP, 128)[:, 0:1]
    for slab in (1, 0):
        total = window_energy(masks, jnp.concatenate([wave_v[slab], edges[slab]], axis=1))
        energy[slab] = gains / jnp.sqrt(total + EPSILON)

    for kind in (0, 1):
        for turn in (0, 2, 1, 3):
            if (kind, turn) != (0, 0):
                finish(kind, turn)
                for slab in (1, 0):
                    multiply(kind, turn, slab)

    result[...] = diagonal_sums(part[1]) * energy[1]
    send("result", result, sibling, arrived)
    out_ref[core] = diagonal_sums(part[0]) * energy[0]
    receive("result", arrived)
    out_ref[1 - core] = arrived[...]
    for made in sent:
        made.wait_send()


def on_device(waveforms, templates, station_mask, channel_order):
    vmem = pl.BlockSpec(memory_space=pltpu.VMEM)
    hbm = pl.BlockSpec(memory_space=pl.ANY)
    slots = 112
    result = pl.pallas_call(
        kernel,
        out_shape=jax.ShapeDtypeStruct((2, GROUP, SLAB), F32),
        in_specs=[hbm] * 4,
        out_specs=vmem,
        scratch_shapes=[
            pltpu.VMEM((2, NZ, WINDOW, LANES), BF16),
            pltpu.VMEM((2, NZ, 8, 128), F32),
            pltpu.VMEM((2, SPAN, LANES), BF16),
            pltpu.VMEM((1, CHANNELS), jnp.int32),
            pltpu.VMEM((1, 160), jnp.int32),
            pltpu.VMEM((CHANNELS, WINDOW), BF16),
            pltpu.VMEM((2, CHANNELS, SLAB), BF16),
            pltpu.VMEM((2, CHANNELS, WINDOW), BF16),
            pltpu.VMEM((2, PADDED, GROUP * STEP), F32),
            pltpu.VMEM((2, GROUP, SLAB), F32),
            pltpu.VMEM((GROUP, SLAB), F32),
            pltpu.VMEM((GROUP, SLAB), F32),
            pltpu.SemaphoreType.DMA((slots,)),
            pltpu.SemaphoreType.DMA((slots,)),
            pltpu.SemaphoreType.DMA((4,)),
        ],
        compiler_params=pltpu.CompilerParams(
            collective_id=0, has_side_effects=True, vmem_limit_bytes=50 * 2**20
        ),
    )(waveforms, templates[0], station_mask, channel_order[None, :])
    return jnp.transpose(result, (1, 0, 2)).reshape(2 * GROUP, SLAB)


def solution(mesh):
    placed = (P(None, ("blk", "tm")), P("blk", None, None), P("blk", None), P())
    return jax.shard_map(
        on_device, mesh=mesh, in_specs=placed, out_specs=P(None, ("blk", "tm")), check_vma=False
    )
```

time: 52.9 us -> 46.7 us (0.88)
  Pallas kernels: 48.9 us -> 43.1 us
    pallas_call x1, Pallas kernels: 48.9 us -> 43.1 us  [on_device(): pl.pallas_call(kernel, out_shape=jax.ShapeDtypeStruct((2, GROUP, SLAB), F...]
where the time goes in v3:
time: 46.7 us; the launch traced here: 46.5 us
  Pallas kernels  43.1 us (92%)
  local copies, waits for them, and re-layouts  3.4 us (7%)
    pallas_call x1, Pallas kernels, on_device(): pl.pallas_call(kernel, out_shape=jax.ShapeDtypeStruct((2, GROUP, SLAB), F...  43.1 us
    unnamed x8, local copies, waits for them, and re-layouts  2.67 us

profile of v3, /device:TPU:1, one launch (start us, length us, event | category | flops | bytes accessed | tf_op | source)
XLA Modules:
  0.0 46.5 jit_solution(17266156059340485269)
XLA Ops:
  0.0 0.0 copy-start.2
  0.0 0.0 copy-start.3
  0.0 0.7 %copy-done.2 = s32[480]{0:T(512)S(1)} copy-done((s32[480]{0:T(512)S(1)}, s32[480]{0:T(512)}, u32[]{:S(2)}) %copy-start.2) | copy-done | bytes 1944
  0.7 0.0 copy-done.3
  0.7 0.0 copy-start
  0.7 1.0 %copy-done = bf16[480,512]{1,0:T(8,128)(2,1)S(1)} copy-done((bf16[480,512]{1,0:T(8,128)(2,1)S(1)}, bf16[480,512]{1,0:T(8,128)(2,1)}, u32[]{:S(2)}) %copy-start) | copy-done | bytes 491544
  1.7 0.0 copy-start.1
  1.7 0.9 %copy-done.1 = bf16[1,480,256]{2,1,0:T(8,128)(2,1)S(1)} copy-done((bf16[1,480,256]{2,1,0:T(8,128)(2,1)S(1)}, bf16[1,480,256]{2,1,0:T(8,128)(2,1)}, u32[]{:S(2)}) %copy-start.1) | copy-done | bytes 245784
  2.7 43.1 %shard_map.46 = f32[2,16,512]{2,1,0:T(8,128)S(1)} custom-call(bf16[480,512]{1,0:T(8,128)(2,1)S(1)} %copy-done, bf16[480,256]{1,0:T(8,128)(2,1)S(1)} %bitcast.4, s32[1,160]{1,0:T(1,128)S(1)} %copy-done.3, s32[1,480]{1,0:T(1,128)S(1)} %bitcast.5), custom_call_target="tpu_custom_call" | custom-call | tf_op jit(solution)/shard_map/pallas_call | solution.py:263
  45.8 0.1 copy.5
  45.8 0.7 %reshape.3 = f32[32,512]{1,0:T(8,128)} reshape(f32[16,2,512]{2,1,0:T(2,128)S(1)} %copy.5) | data formatting | bytes 131072 | tf_op jit(solution)/shard_map/reshape | solution.py:289
Async XLA Ops:
  0.0 0.7 %copy-start.2 = (s32[480]{0:T(512)S(1)}, s32[480]{0:T(512)}, u32[]{:S(2)}) copy-start(s32[480]{0:T(512)} %param.7) | copy-start | bytes 5764
  0.0 0.7 %copy-start.3 = (s32[1,160]{1,0:T(1,128)S(1)}, s32[1,160]{1,0:T(1,128)}, u32[]{:S(2)}) copy-start(s32[1,160]{1,0:T(1,128)} %flag_ref.1) | copy-start | bytes 1924
  0.7 1.0 %copy-start = (bf16[480,512]{1,0:T(8,128)(2,1)S(1)}, bf16[480,512]{1,0:T(8,128)(2,1)}, u32[]{:S(2)}) copy-start(bf16[480,512]{1,0:T(8,128)(2,1)} %wave_ref.1) | copy-start | bytes 1474564
  1.7 0.9 %copy-start.1 = (bf16[1,480,256]{2,1,0:T(8,128)(2,1)S(1)}, bf16[1,480,256]{2,1,0:T(8,128)(2,1)}, u32[]{:S(2)}) copy-start(bf16[1,480,256]{2,1,0:T(8,128)(2,1)} %param.5) | copy-start | bytes 737284

commit v4 on v3

--- a/solution.py
+++ b/solution.py
@@ -140,36 +140,30 @@
         send(("cross", kind, 0), piece(kind, h, 0, cross_turns[kind]), cross)
     send(("cross", "info"), info.at[h, z], cross)
 
-    def to_line(kind, hs, tag):
+    sides = {"own": h, "other": other, "info": both}
+
+    def part_of(kind, tag, dz):
+        return info.at[both, (z - dz + NZ) % NZ] if kind == "info" else piece(kind, sides[tag], dz)
+
+    def to_line(kind, tag):
         for dz in (2, -2, 1, -1):
-            if kind == "info":
-                send((kind, tag, dz), info.at[hs, z], line[dz])
-            else:
-                send((kind, tag, dz), piece(kind, hs, 0), line[dz])
-
-    to_line(0, h, "own")
-    to_line("info", h, "own")
-    to_line(1, h, "own")
+            send((kind, tag, dz), part_of(kind, tag, 0), line[dz])
+
+    to_line(0, "own")
+    to_line(1, "own")
     for turn in (1, 2, 3):
         for kind in (0, 1):
             send(("cross", kind, turn), piece(kind, h, 0, cross_turns[kind] + turn), cross)
 
     plane = {0: [], 1: []}
 
-    def part_of(kind, hs, dz):
-        return info.at[hs, (z - dz + NZ) % NZ] if kind == "info" else piece(kind, hs, dz)
-
-    def zstep(kind, dz):
-        if abs(dz) <= 2:
-            receive((kind, "own", dz), part_of(kind, h, dz))
-            receive((kind, "other", dz), part_of(kind, other, dz))
-        else:
-            receive((kind, "far", dz), part_of(kind, both, dz))
+    def zstep(kind, tag, dz):
+        receive((kind, tag, dz), part_of(kind, tag, dz))
         sign = 1 if dz > 0 else -1
         if abs(dz) == 2:
-            send((kind, "far", 3 * sign), part_of(kind, both, dz), line[sign])
+            send((kind, tag, 3 * sign), part_of(kind, tag, dz), line[sign])
             if sign == (1 if kind == 0 else -1):
-                send((kind, "far", 4), part_of(kind, both, dz), line[2 * sign])
+                send((kind, tag, 4), part_of(kind, tag, dz), line[2 * sign])
         if kind == "info":
             return
         if kind == 0:
@@ -178,8 +172,8 @@
             third = ("west", west, 2) if dz in (2, -1) else ("east", east, 2)
             pushes = (("north", north, 3), ("south", south, 1), third)
         for label, to, turn in pushes:
-            send((kind, label, "plane", dz), piece(kind, both, dz), to)
-            plane[kind].append(((kind, label, "plane", dz), dz, turn))
+            send((kind, label, tag, dz), part_of(kind, tag, dz), to)
+            plane[kind].append(((kind, label, tag, dz), sides[tag], dz, turn))
 
     def multiply(kind, turn, slab, first=False):
         start = 128 * kind + 32 * ((colors[kind] + turn) % 4)
@@ -198,60 +192,75 @@
             part[slab, 0:ROWS, :] += total
 
     def finish(kind, turn):
-        for name, dz, its in plane[kind]:
+        for name, side, dz, its in plane[kind]:
             if its == turn:
-                receive(name, piece(kind, both, dz, turn))
-
-    for kind in (0, 1):
-        receive(("cross", kind, 0), piece(kind, other, 0))
-        to_line(kind, other, "other")
-        if kind == 0:
-            receive(("cross", "info"), info.at[other, z])
-            to_line("info", other, "other")
+                receive(name, piece(kind, side, dz, turn))
+
+    near, far = (2, -2, 1, -1), (3, -3, 4)
+
+    def arrive(kind, tag, steps):
+        for dz in steps:
+            zstep(kind, tag, dz)
+
+    receive(("cross", 0, 0), piece(0, other, 0))
+    to_line(0, "other")
+    receive(("cross", "info"), info.at[other, z])
+    to_line("info", "info")
+    receive(("cross", 1, 0), piece(1, other, 0))
+    to_line(1, "other")
+    arrive(0, "own", near)
+    arrive(1, "own", near)
     xt[0, 0:SLAB, :] = padded_lanes(wave_v[0].T)
     receive("wave", wave_v.at[1])
+    arrive("info", "info", near)
+    arrive(0, "other", near)
+    arrive(0, "own", far)
     xt[1, 0:SLAB, :] = padded_lanes(wave_v[1].T)
-    for step in ((0, 2), (0, -2), ("info", 2), ("info", -2), (0, 1), (0, -1), (1, 2), (1, -2), (1, 1), (1, -1), ("info", 1), ("info", -1)):
-        zstep(*step)
+    arrive(1, "other", near)
     receive("halo", halo_v.at[0])
     send("sib halo", halo_v.at[0], sibling, halo_v.at[1])
     edges = [jnp.where(place == 255, jnp.zeros((), BF16), halo_v[0])]
     xt[0, SLAB:SPAN, :] = padded_lanes(edges[0].T)
-    for step in ((0, 3), (0, -3), (0, 4)):
-        zstep(*step)
-    receive("sib halo", halo_v.at[1])
-    edges.append(jnp.where(place + 8 - 16 * core == 255, jnp.zeros((), BF16), halo_v[1]))
-    xt[1, SLAB:SPAN, :] = padded_lanes(edges[1].T)
-    for turn in (1, 2, 3):
-        receive(("cross", 0, turn), piece(0, other, 0, turn))
-    for slab in (1, 0):
-        multiply(0, 0, slab, True)
-    for step in ((1, 3), (1, -3), (1, 4), ("info", 3), ("info", -3), ("info", 4)):
-        zstep(*step)
-
-    for turn in (1, 2, 3):
-        receive(("cross", 1, turn), piece(1, other, 0, turn))
+    arrive(1, "own", far)
+    arrive("info", "info", far)
     gathered = jnp.concatenate(
         [info[:, :, 0, :].reshape(GROUP, 128), info[:, :, 1, :].reshape(GROUP, 128)], axis=1
     ).astype(BF16)
     masks = jnp.dot(gathered, onehot, preferred_element_type=F32).astype(BF16)[:, :CHANNELS]
     gains = info[:, :, 2, :].reshape(GROUP, 128)[:, 0:1]
-    for slab in (1, 0):
+
+    def set_energy(slab):
         total = window_energy(masks, jnp.concatenate([wave_v[slab], edges[slab]], axis=1))
         energy[slab] = gains / jnp.sqrt(total + EPSILON)
 
-    for kind in (0, 1):
-        for turn in (0, 2, 1, 3):
-            if (kind, turn) != (0, 0):
-                finish(kind, turn)
-                for slab in (1, 0):
-                    multiply(kind, turn, slab)
-
+    set_energy(0)
+    arrive(0, "other", far)
+    arrive(1, "other", far)
+    for turn in (1, 2, 3):
+        receive(("cross", 0, turn), piece(0, other, 0, turn))
+        receive(("cross", 1, turn), piece(1, other, 0, turn))
+    multiply(0, 0, 0, True)
+    receive("sib halo", halo_v.at[1])
+    edges.append(jnp.where(place + 8 - 16 * core == 255, jnp.zeros((), BF16), halo_v[1]))
+    xt[1, SLAB:SPAN, :] = padded_lanes(edges[1].T)
+    multiply(0, 0, 1, True)
+    set_energy(1)
+    chunks = [(kind, turn) for kind in (0, 1) for turn in (0, 2, 1, 3)]
+    for kind, turn in chunks[1:-1]:
+        finish(kind, turn)
+        for slab in (1, 0):
+            multiply(kind, turn, slab)
+    finish(*chunks[-1])
+    multiply(*chunks[-1], 1)
     result[...] = diagonal_sums(part[1]) * energy[1]
     send("result", result, sibling, arrived)
-    out_ref[core] = diagonal_sums(part[0]) * energy[0]
+    multiply(*chunks[-1], 0)
+    own = diagonal_sums(part[0]) * energy[0]
+    for i in range(GROUP):
+        out_ref[pl.ds(2 * i + core, 1), :] = own[i : i + 1]
     receive("result", arrived)
-    out_ref[1 - core] = arrived[...]
+    for i in range(GROUP):
+        out_ref[pl.ds(2 * i + 1 - core, 1), :] = arrived[i : i + 1, :]
     for made in sent:
         made.wait_send()
 
@@ -259,10 +268,10 @@
 def on_device(waveforms, templates, station_mask, channel_order):
     vmem = pl.BlockSpec(memory_space=pltpu.VMEM)
     hbm = pl.BlockSpec(memory_space=pl.ANY)
-    slots = 112
-    result = pl.pallas_call(
+    slots = 160
+    return pl.pallas_call(
         kernel,
-        out_shape=jax.ShapeDtypeStruct((2, GROUP, SLAB), F32),
+        out_shape=jax.ShapeDtypeStruct((2 * GROUP, SLAB), F32),
         in_specs=[hbm] * 4,
         out_specs=vmem,
         scratch_shapes=[
@@ -283,10 +292,9 @@
             pltpu.SemaphoreType.DMA((4,)),
         ],
         compiler_params=pltpu.CompilerParams(
-            collective_id=0, has_side_effects=True, vmem_limit_bytes=50 * 2**20
+            collective_id=0, has_side_effects=True, vmem_limit_bytes=67_043_328
         ),
     )(waveforms, templates[0], station_mask, channel_order[None, :])
-    return jnp.transpose(result, (1, 0, 2)).reshape(2 * GROUP, SLAB)
 
 
 def solution(mesh):

time: 46.7 us -> 44.5 us (0.953)
  local copies, waits for them, and re-layouts: 3.4 us -> 1.47 us
  Pallas kernels: 43.1 us -> 42.6 us
    unnamed x8 -> x1, local copies, waits for them, and re-layouts: 2.67 us -> 1.47 us
    reshape x1 -> x0, local copies, waits for them, and re-layouts: 0.68 us -> none  [on_device(): return jnp.transpose(result, (1, 0, 2)).reshape(2 * GROUP, SLAB)]
where the time goes in v4:
time: 44.5 us; the launch traced here: 44.1 us
  Pallas kernels  42.6 us (96%)
  local copies, waits for them, and re-layouts  1.47 us (3%)
    pallas_call x1, Pallas kernels, on_device(): pl.pallas_call(kernel, out_shape=jax.ShapeDtypeStruct((2 * GROUP, SLAB),...  42.6 us
    unnamed x1, local copies, waits for them, and re-layouts  1.47 us

profile of v4, /device:TPU:1, one launch (start us, length us, event | category | flops | bytes accessed | tf_op | source)
XLA Modules:
  0.0 44.1 jit_solution(5627994864070320638)
XLA Ops:
  0.0 42.6 %shard_map.46 = f32[32,512]{1,0:T(8,128)} custom-call(bf16[480,512]{1,0:T(8,128)(2,1)} %wave_ref.1, bf16[480,256]{1,0:T(8,128)(2,1)} %bitcast.2, s32[1,160]{1,0:T(1,128)} %flag_ref.1, s32[1,480]{1,0:T(1,128)} %bitcast.3), custom_call_target="tpu_custom_call" | custom-call | tf_op jit(solution)/shard_map/pallas_call | solution.py:272
  42.6 1.5 %copy.6 = f32[32,512]{1,0:T(8,128)} copy(f32[32,512]{1,0:T(8,128)} %shard_map.46) | data formatting | bytes 131072

commit v5 on v4

--- a/solution.py
+++ b/solution.py
@@ -114,9 +114,34 @@
     onehot = station_onehot(order)
     flags = jnp.concatenate([flag_v[...].astype(F32), jnp.zeros((1, 96), F32)], axis=1)
     mask_row = jnp.dot(jnp.broadcast_to(flags, (16, 256)).astype(BF16), onehot, preferred_element_type=F32)[0:1]
+    load_wave.wait()
+    pl.semaphore_wait(barrier, len(friends))
+    send("halo", wave_v.at[0, :, pl.ds(0, WINDOW)], before, halo_v.at[0])
+    send("wave", wave_v.at[0], sibling, wave_v.at[1])
     load_tpl.wait()
     masked = padded_lanes(tpl_v[...].T) * mask_row.astype(BF16)
     g[h, z] = masked
+    def rows(kind, turn):
+        return pl.ds(pl.multiple_of(128 * kind + 32 * ((colors[kind] + turn) % 4), 32), 32)
+
+    def piece(kind, hs, dz, turn=0):
+        return g.at[hs, (z - dz + NZ) % NZ, rows(kind, turn), :]
+
+    both = pl.ds(0, 2)
+    for kind in (0, 1):
+        send(("cross", kind, 0), piece(kind, h, 0, cross_turns[kind]), cross)
+
+    sides = {"own": h, "other": other, "info": both}
+
+    def part_of(kind, tag, dz):
+        return info.at[both, (z - dz + NZ) % NZ] if kind == "info" else piece(kind, sides[tag], dz)
+
+    def to_line(kind, tag):
+        for dz in (2, -2, 1, -1):
+            send((kind, tag, dz), part_of(kind, tag, 0), line[dz])
+
+    to_line(0, "own")
+    to_line(1, "own")
     wide = masked.astype(F32)
     norm = jnp.sum(jnp.sum(wide * wide, axis=0, keepdims=True), axis=1, keepdims=True)
     live = jnp.sum(mask_row, axis=1, keepdims=True)
@@ -124,33 +149,7 @@
     info[h, z] = jnp.concatenate(
         [flags[:, :128], flags[:, 128:], jnp.broadcast_to(scale, (1, 128)), jnp.zeros((5, 128), F32)], axis=0
     )
-    load_wave.wait()
-    pl.semaphore_wait(barrier, len(friends))
-
-    def rows(kind, turn):
-        return pl.ds(pl.multiple_of(128 * kind + 32 * ((colors[kind] + turn) % 4), 32), 32)
-
-    def piece(kind, hs, dz, turn=0):
-        return g.at[hs, (z - dz + NZ) % NZ, rows(kind, turn), :]
-
-    both = pl.ds(0, 2)
-    send("halo", wave_v.at[0, :, pl.ds(0, WINDOW)], before, halo_v.at[0])
-    send("wave", wave_v.at[0], sibling, wave_v.at[1])
-    for kind in (0, 1):
-        send(("cross", kind, 0), piece(kind, h, 0, cross_turns[kind]), cross)
     send(("cross", "info"), info.at[h, z], cross)
-
-    sides = {"own": h, "other": other, "info": both}
-
-    def part_of(kind, tag, dz):
-        return info.at[both, (z - dz + NZ) % NZ] if kind == "info" else piece(kind, sides[tag], dz)
-
-    def to_line(kind, tag):
-        for dz in (2, -2, 1, -1):
-            send((kind, tag, dz), part_of(kind, tag, 0), line[dz])
-
-    to_line(0, "own")
-    to_line(1, "own")
     for turn in (1, 2, 3):
         for kind in (0, 1):
             send(("cross", kind, turn), piece(kind, h, 0, cross_turns[kind] + turn), cross)
@@ -167,9 +166,9 @@
         if kind == "info":
             return
         if kind == 0:
-            pushes = (("east", east, 3), ("west", west, 1), (("cross y", cross, 2) if dz in (2, 1) else ("mate", mate, 2)))
+            pushes = (("east", east, 3), ("west", west, 1), (("cross y", cross, 2) if dz in (-3, 4) else ("mate", mate, 2)))
         else:
-            third = ("west", west, 2) if dz in (2, -1) else ("east", east, 2)
+            third = ("west", west, 2) if dz in (-3, 4, -1) else ("east", east, 2)
             pushes = (("north", north, 3), ("south", south, 1), third)
         for label, to, turn in pushes:
             send((kind, label, tag, dz), part_of(kind, tag, dz), to)
@@ -214,9 +213,9 @@
     receive("wave", wave_v.at[1])
     arrive("info", "info", near)
     arrive(0, "other", near)
-    arrive(0, "own", far)
     xt[1, 0:SLAB, :] = padded_lanes(wave_v[1].T)
     arrive(1, "other", near)
+    arrive(0, "own", far)
     receive("halo", halo_v.at[0])
     send("sib halo", halo_v.at[0], sibling, halo_v.at[1])
     edges = [jnp.where(place == 255, jnp.zeros((), BF16), halo_v[0])]
@@ -235,6 +234,7 @@
 
     set_energy(0)
     arrive(0, "other", far)
+    early = len(sent)
     arrive(1, "other", far)
     for turn in (1, 2, 3):
         receive(("cross", 0, turn), piece(0, other, 0, turn))
@@ -247,6 +247,9 @@
     set_energy(1)
     chunks = [(kind, turn) for kind in (0, 1) for turn in (0, 2, 1, 3)]
     for kind, turn in chunks[1:-1]:
+        if (kind, turn) == (1, 2):
+            for made in sent[:early]:
+                made.wait_send()
         finish(kind, turn)
         for slab in (1, 0):
             multiply(kind, turn, slab)
@@ -261,7 +264,7 @@
     receive("result", arrived)
     for i in range(GROUP):
         out_ref[pl.ds(2 * i + 1 - core, 1), :] = arrived[i : i + 1, :]
-    for made in sent:
+    for made in sent[early:]:
         made.wait_send()
 
 

time: 44.5 us -> 44.3 us (level)
  no operation moved by 1% of the time
where the time goes in v5:
time: 44.3 us; the launch traced here: 44.2 us
  Pallas kernels  42.7 us (96%)
  local copies, waits for them, and re-layouts  1.47 us (3%)
    pallas_call x1, Pallas kernels, on_device(): pl.pallas_call(kernel, out_shape=jax.ShapeDtypeStruct((2 * GROUP, SLAB),...  42.7 us
    unnamed x1, local copies, waits for them, and re-layouts  1.47 us

profile of v5, /device:TPU:1, one launch (start us, length us, event | category | flops | bytes accessed | tf_op | source)
XLA Modules:
  0.0 44.2 jit_solution(9269347820842149126)
XLA Ops:
  0.0 42.7 %shard_map.46 = f32[32,512]{1,0:T(8,128)} custom-call(bf16[480,512]{1,0:T(8,128)(2,1)} %wave_ref.1, bf16[480,256]{1,0:T(8,128)(2,1)} %bitcast.2, s32[1,160]{1,0:T(1,128)} %flag_ref.1, s32[1,480]{1,0:T(1,128)} %bitcast.3), custom_call_target="tpu_custom_call" | custom-call | tf_op jit(solution)/shard_map/pallas_call | solution.py:275
  42.7 1.5 %copy.6 = f32[32,512]{1,0:T(8,128)} copy(f32[32,512]{1,0:T(8,128)} %shard_map.46) | data formatting | bytes 131072

commit v6 on v5

--- a/solution.py
+++ b/solution.py
@@ -174,7 +174,7 @@
             send((kind, label, tag, dz), part_of(kind, tag, dz), to)
             plane[kind].append(((kind, label, tag, dz), sides[tag], dz, turn))
 
-    def multiply(kind, turn, slab, first=False):
+    def multiply(kind, turn, slab, first=False, last=False):
         start = 128 * kind + 32 * ((colors[kind] + turn) % 4)
         total = None
         for half in (0, STEP):
@@ -184,9 +184,11 @@
                 xt[slab, pl.ds(at, ROWS), :], tpl, (((1,), (1,)), ((), ())), preferred_element_type=F32
             )
             total = term if total is None else total + term
+        if last:
+            rest = jnp.zeros((PADDED - ROWS, GROUP * STEP), F32)
+            return diagonal_sums(jnp.concatenate([part[slab, 0:ROWS, :] + total, rest], axis=0)) * energy[slab]
         if first:
             part[slab, 0:ROWS, :] = total
-            part[slab, ROWS:PADDED, :] = jnp.zeros((PADDED - ROWS, GROUP * STEP), F32)
         else:
             part[slab, 0:ROWS, :] += total
 
@@ -254,11 +256,9 @@
         for slab in (1, 0):
             multiply(kind, turn, slab)
     finish(*chunks[-1])
-    multiply(*chunks[-1], 1)
-    result[...] = diagonal_sums(part[1]) * energy[1]
+    result[...] = multiply(*chunks[-1], 1, last=True)
     send("result", result, sibling, arrived)
-    multiply(*chunks[-1], 0)
-    own = diagonal_sums(part[0]) * energy[0]
+    own = multiply(*chunks[-1], 0, last=True)
     for i in range(GROUP):
         out_ref[pl.ds(2 * i + core, 1), :] = own[i : i + 1]
     receive("result", arrived)

time: 44.3 us -> 44.3 us (level)
  no operation moved by 1% of the time
where the time goes in v6:
time: 44.3 us; the launch traced here: 44.2 us
  Pallas kernels  42.7 us (96%)
  local copies, waits for them, and re-layouts  1.47 us (3%)
    pallas_call x1, Pallas kernels, on_device(): pl.pallas_call(kernel, out_shape=jax.ShapeDtypeStruct((2 * GROUP, SLAB),...  42.7 us
    unnamed x1, local copies, waits for them, and re-layouts  1.47 us

profile of v6, /device:TPU:1, one launch (start us, length us, event | category | flops | bytes accessed | tf_op | source)
XLA Modules:
  0.0 44.2 jit_solution(9269347820842149126)
XLA Ops:
  0.0 42.7 %shard_map.46 = f32[32,512]{1,0:T(8,128)} custom-call(bf16[480,512]{1,0:T(8,128)(2,1)} %wave_ref.1, bf16[480,256]{1,0:T(8,128)(2,1)} %bitcast.2, s32[1,160]{1,0:T(1,128)} %flag_ref.1, s32[1,480]{1,0:T(1,128)} %bitcast.3), custom_call_target="tpu_custom_call" | custom-call | tf_op jit(solution)/shard_map/pallas_call | solution.py:275
  42.7 1.5 %copy.6 = f32[32,512]{1,0:T(8,128)} copy(f32[32,512]{1,0:T(8,128)} %shard_map.46) | data formatting | bytes 131072
